TPU v7x, 256 devices: a whole 4x4x8 slice. The times are simulated.
256 devices in a mesh: space: 16 (over x_hi, z), chan: 16 (over y, x_lo, core).
Axes of the slice: x: 4 (x_hi: 2, x_lo: 2; x = x_hi * 2 + x_lo), y: 4, z: 8, core: 2. Of those that a mesh axis runs over, the one named last changes fastest.
Arguments:
- activations: bfloat16 [512, 128, 16, 128], P('chan', 'space'), may hold values from -6 to 6
- out_grad: bfloat16 [512, 128, 16, 128], P('chan', 'space'), may hold values from -6 to 6
Outputs:
- filter_grad: float32 [27, 512, 512], P(None, 'space', 'chan')
All inputs are finite; a program needn't handle non-finite values.
Results may differ from a plain program's by a relative error of at most 0.0003.
Values may be sent and summed in bfloat16 or wider, within the bound.
No kernel may reach another device: no remote copies, remote signals or barrier semaphores. Data moves between devices by JAX's collectives and lax.ppermute only.
A program may use at most 192 MiB of HBM per device.

v0:
```python
import functools

import jax
import jax.numpy as jnp
from jax import lax
from jax.experimental import pallas as pl
from jax.experimental.pallas import tpu as pltpu
from jax.sharding import PartitionSpec as P


AXES = ("space", "chan")
VMEM = 52 * 2**20
SIZES = (("h", 2), ("z", 8), ("y", 4), ("x", 2), ("k", 2))


def place(index):
    found = {}
    for name, size in reversed(SIZES):
        index, found[name] = divmod(index, size)
    return found


def index_of(found):
    index = 0
    for name, size in SIZES:
        index = index * size + found[name] % size
    return index


def send(value, move):
    pairs = [(i, index_of(move(place(i)))) for i in range(256)]
    return lax.ppermute(value, AXES, pairs)


def shift(value, **steps):
    return send(value, lambda d: {n: d[n] + steps.get(n, 0) for n in d})


def spread_body(size_z, slabs, lanes, middle, edge, out_ref):
    rows = middle.shape[0]
    z = lax.broadcasted_iota(jnp.int32, (rows, lanes), 1) % size_z
    blank = jnp.zeros((size_z, out_ref.shape[2]), out_ref.dtype)
    for part in range(out_ref.shape[0]):
        x = pl.program_id(0) * out_ref.shape[0] + part
        inside = jnp.logical_and(x > 0, x <= slabs)
        at = pl.multiple_of(jnp.clip(x - 1, 0, slabs - 1) * lanes, lanes)
        side = pl.multiple_of(x // (slabs + 1) * lanes, lanes)
        center = jnp.where(
            inside,
            middle[:, pl.ds(at, lanes)].astype(jnp.float32),
            edge[:, pl.ds(side, lanes)].astype(jnp.float32),
        )
        below = jnp.where(z == 0, 0.0, pltpu.roll(center, 1, 1))
        above = jnp.where(z == size_z - 1, 0.0, pltpu.roll(center, lanes - 1, 1))
        stack = [below, center, above, jnp.zeros((rows, lanes), jnp.float32)]
        turned = jnp.concatenate(stack, axis=0).T.astype(out_ref.dtype)
        out_ref[part, :size_z] = blank
        out_ref[part, size_z : size_z + lanes] = turned
        out_ref[part, size_z + lanes :] = blank


def spread(cells, edges, size_z, lanes):
    rows, total = cells.shape
    slabs = total // lanes
    shape = (slabs + 2, lanes + 2 * size_z, 4 * rows)
    return pl.pallas_call(
        functools.partial(spread_body, size_z, slabs, lanes),
        grid=((slabs + 2) // 2,),
        in_specs=[
            pl.BlockSpec(cells.shape, lambda x: (0, 0)),
            pl.BlockSpec(edges.shape, lambda x: (0, 0)),
        ],
        out_specs=pl.BlockSpec((2,) + shape[1:], lambda x: (x, 0, 0)),
        out_shape=jax.ShapeDtypeStruct(shape, cells.dtype),
        compiler_params=pltpu.CompilerParams(vmem_limit_bytes=VMEM),
        cost_estimate=pl.CostEstimate(
            flops=10 * 2**20, bytes_accessed=10 * 2**20, transcendentals=0
        ),
    )(cells, edges)


def product_body(cuts, slabs, size_z, *refs):
    count = len(cuts)
    refs = list(refs)
    blocks = [[refs.pop(0) for _ in range(cut)] for cut in cuts]
    own, near, out_ref, held, total, sems = refs
    x = pl.program_id(0)
    lanes = held.shape[1] // slabs
    rows = held.shape[0] // count
    tall = count * rows

    @pl.when(x == 0)
    def _():
        copies = []
        for i, parts in enumerate(blocks):
            width = held.shape[1] // len(parts)
            for j, part in enumerate(parts):
                to = held.at[pl.ds(i * rows, rows), pl.ds(j * width, width)]
                copies.append(pltpu.make_async_copy(part, to, sems.at[len(copies)]))
        for copy in copies:
            copy.start()
        total[...] = jnp.zeros_like(total)
        for copy in copies:
            copy.wait()

    def add(first, last):
        left = jnp.concatenate(
            [
                held[:, pl.ds(pl.multiple_of((x - a) * lanes, lanes), lanes)]
                for a in range(first, last)
            ],
            axis=0,
        )
        for b in range(3):
            at = slice(b * size_z, b * size_z + lanes)
            total[b, first * tall : last * tall] += jnp.dot(
                left,
                jnp.concatenate([own[0, at, :], near[0, at, :]], axis=1),
                preferred_element_type=jnp.float32,
            )

    for first, last, chosen in (
        (0, 1, x == 0),
        (0, 2, x == 1),
        (0, 3, jnp.logical_and(x > 1, x < slabs)),
        (1, 3, x == slabs),
        (2, 3, x == slabs + 1),
    ):
        pl.when(chosen)(functools.partial(add, first, last))

    @pl.when(x == slabs + 1)
    def _():
        for block in range(count):
            for n in range(2):
                for a in range(3):
                    for b in range(3):
                        at = a * tall + block * rows
                        to = (3 * a + b) * 96
                        out_ref[block, n, :, to : to + 96] = total[
                            b, at : at + rows, n * 128 : n * 128 + 96
                        ]
                out_ref[block, n, :, 864:] = jnp.zeros((rows, 32), jnp.float32)


def product(blocks, own, near, size_z):
    count = len(blocks)
    rows = blocks[0][0].shape[0]
    slabs = own.shape[0] - 2
    cells = slabs * (own.shape[1] - 2 * size_z)
    cuts = tuple(len(parts) for parts in blocks)
    field = pl.BlockSpec((1,) + own.shape[1:], lambda x: (x, 0, 0))
    return pl.pallas_call(
        functools.partial(product_body, cuts, slabs, size_z),
        grid=(slabs + 2,),
        in_specs=[pl.BlockSpec(memory_space=pl.ANY)] * sum(cuts) + [field, field],
        out_specs=pl.BlockSpec((count, 2, rows, 896), lambda x: (0, 0, 0, 0)),
        out_shape=jax.ShapeDtypeStruct((count, 2, rows, 896), jnp.float32),
        scratch_shapes=[
            pltpu.VMEM((count * rows, cells), own.dtype),
            pltpu.VMEM((3, 3 * count * rows, 2 * own.shape[2]), jnp.float32),
            pltpu.SemaphoreType.DMA((sum(cuts),)),
        ],
        compiler_params=pltpu.CompilerParams(vmem_limit_bytes=VMEM),
        cost_estimate=pl.CostEstimate(
            flops=count * 3 * 10**9, bytes_accessed=16 * 2**20, transcendentals=0
        ),
    )(*[part for parts in blocks for part in parts], own, near)


def ring_sum(piece):
    up, down = piece(4), piece(-3)
    for step in (3, 2, 1):
        up = shift(up, z=1) + piece(step)
        if step > 1:
            down = shift(down, z=-1) + piece(1 - step)
        up, down = lax.optimization_barrier((up, down))
    return shift(up, z=1) + shift(down, z=-1) + piece(0)


def shards(activations, out_grad):
    count, slab_x, size_y, size_z = activations.shape
    lanes = size_y * size_z
    cells = slab_x * lanes
    half = cells // 2
    space, chan = lax.axis_index("space"), lax.axis_index("chan")
    z, high = space % 8, space // 8
    y, x, k = chan // 4, chan // 2 % 2, chan % 2

    def cross(value, bits):
        return send(value, lambda d: dict(d, y=d["y"] ^ bits))

    cut = slab_x // 2
    one = out_grad[:, :cut].reshape(count, half)
    one, out_grad = lax.optimization_barrier((one, out_grad))
    next_one = cross(one, 1)
    two = out_grad[:, cut:].reshape(count, half)
    two, activations = lax.optimization_barrier((two, activations))
    last_two = cross(two, 3)
    next_two, last_one = cross(two, 1), cross(one, 3)
    acts = activations.reshape(count, cells)
    acts_near = send(acts, lambda d: dict(d, x=d["x"] ^ 1))

    def ends(flip):
        def move(value, step):
            pairs = []
            for i in range(256):
                d = place(i)
                space_to = d["h"] * 8 + d["z"] + step
                if 0 <= space_to < 16:
                    to = dict(d, h=space_to // 8, z=space_to % 8, x=d["x"] ^ flip)
                    pairs.append((i, index_of(to)))
            return lax.ppermute(value, AXES, pairs)

        return move(acts[:, cells - lanes :], 1), move(acts[:, :lanes], -1)

    own_ends, near_ends = ends(0), ends(1)
    next_one, last_two, own_ends = lax.optimization_barrier((next_one, last_two, own_ends))
    far_one, far_two = cross(next_one, 3), cross(last_two, 1)
    own = spread(acts, jnp.concatenate(own_ends, axis=1), size_z, lanes)
    next_one, last_two, next_two, last_one, own = lax.optimization_barrier(
        (next_one, last_two, next_two, last_one, own)
    )
    mates = [shift(v, k=1) for v in (one, two, next_one, last_two, next_two, last_one)]
    far_one, far_two, acts_near, near_ends, own, mates = lax.optimization_barrier(
        (far_one, far_two, acts_near, near_ends, own, mates)
    )
    far_mate = shift(far_one, k=1), shift(far_two, k=1)
    near = spread(acts_near, jnp.concatenate(near_ends, axis=1), size_z, lanes)
    blocks = (
        (one, two),
        (mates[0], mates[1]),
        (next_one, next_two),
        (mates[2], mates[4]),
        (far_one, far_two),
        far_mate,
        (last_one, last_two),
        (mates[5], mates[3]),
    )
    parts = product(blocks, own, near, size_z)

    def piece(step):
        to = lax.rem(z + step + 8, 8)
        b, j, c = to // 4, to // 2 % 2, to % 2
        at = (0, (b ^ (y % 2)) * 2 + (c ^ k), j ^ x, 0, 0)
        split = parts.reshape((2, 4) + parts.shape[1:])
        return lax.dynamic_slice(split, at, (2, 1, 1) + parts.shape[2:])[:, 0, 0]

    mine = ring_sum(piece)
    here = (high == y // 2).astype(jnp.int32)
    keep = lax.dynamic_index_in_dim(mine, 1 - here, 0, False)
    give = lax.dynamic_index_in_dim(mine, here, 0, False)

    def turned(d, flip):
        bits = d["z"]
        low = bits // 2 % 2
        return dict(d, z=bits + 2 * (d["x"] - low), x=low, h=d["h"] + flip)

    total = send(keep, lambda d: turned(d, 0)) + send(give, lambda d: turned(d, 1))
    scale = jnp.float32(1.0) / jnp.sqrt(jnp.float32(cells * lax.axis_size("space")))
    total = (total[:, : 27 * count] * scale).reshape(count, 27, count)
    return jnp.transpose(total, (1, 0, 2))


def solution(mesh):
    return jax.shard_map(
        shards,
        mesh=mesh,
        in_specs=(P("chan", "space", None, None), P("chan", "space", None, None)),
        out_specs=P(None, "space", "chan"),
        check_vma=False,
    )
```

profile of v0, /device:TPU:2, one launch (start us, length us, event | category | flops | bytes accessed | tf_op | source)
XLA Modules:
  0.0 144.3 jit_solution(12757912446300612391)
XLA Ops:
  0.0 1.1 slice.17
  1.2 0.3 copy.12
  1.5 0.3 copy.11
  1.9 3.1 %collective-permute-start.1 = (bf16[32,8192]{1,0:T(8,128)(2,1)S(1)}, bf16[32,8192]{1,0:T(8,128)(2,1)S(1)}, u32[]{:S(2)}, u32[]{:S(2)}) collective-permute-start(bf16[32,8192]{1,0:T(8,128)(2,1)S(1)} %bitcast.44), channel_id=1, source_target_pairs={{0,12},{1,13},{2,14},{3,15},{4,8},{5,9},{6,10},{7,11},{8,4},{9,5},... | collective-permute-start | bytes 1572872 | tf_op jit(solution)/shard_map/ppermute | solution.py:32
  5.1 1.9 %collective-permute-start = (bf16[32,8192]{1,0:T(8,128)(2,1)S(1)}, bf16[32,8192]{1,0:T(8,128)(2,1)S(1)}, u32[]{:S(2)}, u32[]{:S(2)}) collective-permute-start(bf16[32,8192]{1,0:T(8,128)(2,1)S(1)} %bitcast.40), channel_id=1, source_target_pairs={{0,4},{1,5},{2,6},{3,7},{4,0},{5,1},{6,2},{7,3},{8,12},{9,13},{10,... | collective-permute-start | bytes 1572872 | tf_op jit(solution)/shard_map/ppermute | solution.py:32
  7.0 0.2 collective-permute-start.10
  7.2 0.7 copy.10
  7.9 3.8 %collective-permute-start.2 = (bf16[32,2048]{1,0:T(8,128)(2,1)S(1)}, bf16[32,2048]{1,0:T(8,128)(2,1)S(1)}, u32[]{:S(2)}, u32[]{:S(2)}) collective-permute-start(bf16[32,2048]{1,0:T(8,128)(2,1)S(1)} %get-tuple-element.74), channel_id=1, source_target_pairs={{0,16},{1,17},{2,18},{3,19},{4,20},{5,21},{6,22},{7,23},{8,24},{9,... | collective-permute-start | bytes 393224 | tf_op jit(solution)/shard_map/ppermute | solution.py:212
  11.8 2.5 %collective-permute-done.2 = bf16[32,2048]{1,0:T(8,128)(2,1)S(1)} collective-permute-done((bf16[32,2048]{1,0:T(8,128)(2,1)S(1)}, bf16[32,2048]{1,0:T(8,128)(2,1)S(1)}, u32[]{:S(2)}, u32[]{:S(2)}) %collective-permute-start.2) | collective-permute-done | bytes 131104 | tf_op jit(solution)/shard_map/ppermute | solution.py:212
  14.3 1.3 collective-permute-start.3
  15.6 6.0 %collective-permute-done.3 = bf16[32,2048]{1,0:T(8,128)(2,1)S(1)} collective-permute-done((bf16[32,2048]{1,0:T(8,128)(2,1)S(1)}, bf16[32,2048]{1,0:T(8,128)(2,1)S(1)}, u32[]{:S(2)}, u32[]{:S(2)}) %collective-permute-start.3) | collective-permute-done | bytes 131104 | tf_op jit(solution)/shard_map/ppermute | solution.py:212
  21.6 3.9 %collective-permute-start.7 = (bf16[32,2048]{1,0:T(8,128)(2,1)S(1)}, bf16[32,2048]{1,0:T(8,128)(2,1)S(1)}, u32[]{:S(2)}, u32[]{:S(2)}) collective-permute-start(bf16[32,2048]{1,0:T(8,128)(2,1)S(1)} %get-tuple-element.74), channel_id=1, source_target_pairs={{0,18},{1,19},{2,16},{3,17},{4,22},{5,23},{6,20},{7,21},{8,26},{9,... | collective-permute-start | bytes 393224 | tf_op jit(solution)/shard_map/ppermute | solution.py:212
  25.4 4.1 %collective-permute-done.refs_4_ = bf16[32,8192]{1,0:T(8,128)(2,1)S(1)} collective-permute-done((bf16[32,8192]{1,0:T(8,128)(2,1)S(1)}, bf16[32,8192]{1,0:T(8,128)(2,1)S(1)}, u32[]{:S(2)}, u32[]{:S(2)}) %collective-permute-start) | collective-permute-done | bytes 524320 | tf_op jit(solution)/shard_map/ppermute | solution.py:32
  29.6 1.3 collective-permute-start.8
  31.0 0.6 collective-permute-start.6
  31.6 5.8 %collective-permute-done.8 = bf16[32,2048]{1,0:T(8,128)(2,1)S(1)} collective-permute-done((bf16[32,2048]{1,0:T(8,128)(2,1)S(1)}, bf16[32,2048]{1,0:T(8,128)(2,1)S(1)}, u32[]{:S(2)}, u32[]{:S(2)}) %collective-permute-start.8) | collective-permute-done | bytes 131104 | tf_op jit(solution)/shard_map/ppermute | solution.py:212
  37.5 0.5 collective-permute-start.4
  37.9 0.2 collective-permute-start.5
  38.2 4.7 %shard_map.28.refs_16_ = bf16[10,2304,128]{2,1,0:T(8,128)(2,1)} custom-call(bf16[32,16384]{1,0:T(8,128)(2,1)S(1)} %bitcast.39, bf16[32,4096]{1,0:T(8,128)(2,1)S(1)} %pad_maximum_fusion.edge), custom_call_target="tpu_custom_call" | custom-call | flops 10485760 | bytes 10485760 | tf_op jit(solution)/shard_map/pallas_call | solution.py:66
  42.9 0.6 collective-permute-start.14
  43.5 9.6 %collective-permute-done.4.refs_8_ = bf16[32,8192]{1,0:T(8,128)(2,1)} collective-permute-done((bf16[32,8192]{1,0:T(8,128)(2,1)S(1)}, bf16[32,8192]{1,0:T(8,128)(2,1)}, u32[]{:S(2)}, u32[]{:S(2)}) %collective-permute-start.4) | collective-permute-done | bytes 524320 | tf_op jit(solution)/shard_map/ppermute | solution.py:32
  53.1 0.5 collective-permute-start.16
  53.6 5.3 %collective-permute-done.6.middle = bf16[32,16384]{1,0:T(8,128)(2,1)S(1)} collective-permute-done((bf16[32,16384]{1,0:T(8,128)(2,1)S(1)}, bf16[32,16384]{1,0:T(8,128)(2,1)S(1)}, u32[]{:S(2)}, u32[]{:S(2)}) %collective-permute-start.6) | collective-permute-done | bytes 1048608 | tf_op jit(solution)/shard_map/ppermute | solution.py:32
  59.2 0.6 copy-done.7
  60.0 0.2 copy-done.9
  60.1 0.2 copy-done.10
  60.3 4.6 %shard_map.29.refs_17_ = bf16[10,2304,128]{2,1,0:T(8,128)(2,1)} custom-call(bf16[32,16384]{1,0:T(8,128)(2,1)S(1)} %collective-permute-done.6.middle, bf16[32,4096]{1,0:T(8,128)(2,1)S(1)} %pad_maximum_fusion.1.edge), custom_call_target="tpu_custom_call" | custom-call | flops 10485760 | bytes 10485760 | tf_op jit(solution)/shard_map/pallas_call | solution.py:66
  65.0 0.8 copy-done.11
  65.8 27.4 %shard_map.30 = f32[8,2,32,896]{3,2,1,0:T(8,128)} custom-call(bf16[32,8192]{1,0:T(8,128)(2,1)S(1)} %bitcast.43, bf16[32,8192]{1,0:T(8,128)(2,1)S(1)} %bitcast.47, bf16[32,8192]{1,0:T(8,128)(2,1)S(1)} %collective-permute-done.11.refs_2_, bf16[32,8192]{1,0:T(8,128)(2,1)} %copy-done.6, bf16[32,8192]{1,0:T(8,128)(2,1)} %copy-done.4, bf16[32,8192]{1,0:T(8,128)(2,1)} %copy-done.3, ...), custom_call_target="tpu_custom_call" | custom-call | flops 24000000000 | bytes 16777216 | tf_op jit(solution)/shard_map/pallas_call | solution.py:152
  93.2 1.2 dynamic-slice_bitcast_fusion
  94.5 5.8 %collective-permute-start.20 = (f32[2,32,896]{2,1,0:T(8,128)S(1)}, f32[2,32,896]{2,1,0:T(8,128)S(1)}, u32[]{:S(2)}, u32[]{:S(2)}) collective-permute-start(f32[2,32,896]{2,1,0:T(8,128)S(1)} %get-tuple-element.71), channel_id=1, source_target_pairs={{0,112},{1,113},{2,114},{3,115},{4,116},{5,117},{6,118},{7,119},{8... | collective-permute-start | bytes 688136 | tf_op jit(solution)/shard_map/ppermute | solution.py:32
  100.2 5.0 %collective-permute-done.20 = f32[2,32,896]{2,1,0:T(8,128)S(1)} collective-permute-done((f32[2,32,896]{2,1,0:T(8,128)S(1)}, f32[2,32,896]{2,1,0:T(8,128)S(1)}, u32[]{:S(2)}, u32[]{:S(2)}) %collective-permute-start.20) | collective-permute-done | bytes 229408 | tf_op jit(solution)/shard_map/ppermute | solution.py:32
  105.3 3.4 %collective-permute-done.19 = f32[2,32,896]{2,1,0:T(8,128)S(1)} collective-permute-done((f32[2,32,896]{2,1,0:T(8,128)S(1)}, f32[2,32,896]{2,1,0:T(8,128)S(1)}, u32[]{:S(2)}, u32[]{:S(2)}) %collective-permute-start.19) | collective-permute-done | bytes 229408 | tf_op jit(solution)/shard_map/ppermute | solution.py:32
  108.7 1.1 bitcast_add_fusion.4
  109.8 0.7 collective-permute-start.22
  110.4 1.5 %collective-permute-start.21 = (f32[2,32,896]{2,1,0:T(8,128)S(1)}, f32[2,32,896]{2,1,0:T(8,128)S(1)}, u32[]{:S(2)}, u32[]{:S(2)}) collective-permute-start(f32[2,32,896]{2,1,0:T(8,128)S(1)} %get-tuple-element.61), channel_id=1, source_target_pairs={{0,16},{1,17},{2,18},{3,19},{4,20},{5,21},{6,22},{7,23},{8,24},{9,... | collective-permute-start | bytes 688136 | tf_op jit(solution)/shard_map/ppermute | solution.py:32
  111.9 4.4 %collective-permute-done.22 = f32[2,32,896]{2,1,0:T(8,128)S(1)} collective-permute-done((f32[2,32,896]{2,1,0:T(8,128)S(1)}, f32[2,32,896]{2,1,0:T(8,128)S(1)}, u32[]{:S(2)}, u32[]{:S(2)}) %collective-permute-start.22) | collective-permute-done | bytes 229408 | tf_op jit(solution)/shard_map/ppermute | solution.py:32
  116.2 1.5 %collective-permute-done.21 = f32[2,32,896]{2,1,0:T(8,128)S(1)} collective-permute-done((f32[2,32,896]{2,1,0:T(8,128)S(1)}, f32[2,32,896]{2,1,0:T(8,128)S(1)}, u32[]{:S(2)}, u32[]{:S(2)}) %collective-permute-start.21) | collective-permute-done | bytes 229408 | tf_op jit(solution)/shard_map/ppermute | solution.py:32
  117.8 0.3 collective-permute-start.23
  118.1 7.0 %collective-permute-done.23 = f32[2,32,896]{2,1,0:T(8,128)S(1)} collective-permute-done((f32[2,32,896]{2,1,0:T(8,128)S(1)}, f32[2,32,896]{2,1,0:T(8,128)S(1)}, u32[]{:S(2)}, u32[]{:S(2)}) %collective-permute-start.23) | collective-permute-done | bytes 229408 | tf_op jit(solution)/shard_map/ppermute | solution.py:32
  125.2 3.2 %collective-permute-start.25 = (f32[2,32,896]{2,1,0:T(8,128)S(1)}, f32[2,32,896]{2,1,0:T(8,128)S(1)}, u32[]{:S(2)}, u32[]{:S(2)}) collective-permute-start(f32[2,32,896]{2,1,0:T(8,128)S(1)} %get-tuple-element.66), channel_id=1, source_target_pairs={{0,112},{1,113},{2,114},{3,115},{4,116},{5,117},{6,118},{7,119},{8... | collective-permute-start | bytes 688136 | tf_op jit(solution)/shard_map/ppermute | solution.py:32
  128.5 4.0 %collective-permute-done.24 = f32[2,32,896]{2,1,0:T(8,128)S(1)} collective-permute-done((f32[2,32,896]{2,1,0:T(8,128)S(1)}, f32[2,32,896]{2,1,0:T(8,128)S(1)}, u32[]{:S(2)}, u32[]{:S(2)}) %collective-permute-start.24) | collective-permute-done | bytes 229408 | tf_op jit(solution)/shard_map/ppermute | solution.py:32
  132.5 2.1 %collective-permute-start.27 = (f32[32,896]{1,0:T(8,128)S(1)}, f32[32,896]{1,0:T(8,128)S(1)}, u32[]{:S(2)}, u32[]{:S(2)}) collective-permute-start(f32[32,896]{1,0:T(8,128)S(1)} %get-tuple-element.76), channel_id=1, source_target_pairs={{0,128},{1,129},{2,160},{3,161},{4,132},{5,133},{6,164},{7,165},{8... | collective-permute-start | bytes 344072 | tf_op jit(solution)/shard_map/ppermute | solution.py:32
  134.6 5.4 %collective-permute-start.26 = (f32[32,896]{1,0:T(8,128)S(1)}, f32[32,896]{1,0:T(8,128)S(1)}, u32[]{:S(2)}, u32[]{:S(2)}) collective-permute-start(f32[32,896]{1,0:T(8,128)S(1)} %get-tuple-element.75), channel_id=1, source_target_pairs={{0,0},{1,1},{2,32},{3,33},{4,4},{5,5},{6,36},{7,37},{8,8},{9,9},{1... | collective-permute-start | bytes 344072 | tf_op jit(solution)/shard_map/ppermute | solution.py:32
  140.0 1.7 %collective-permute-done.27 = f32[32,896]{1,0:T(8,128)S(1)} collective-permute-done((f32[32,896]{1,0:T(8,128)S(1)}, f32[32,896]{1,0:T(8,128)S(1)}, u32[]{:S(2)}, u32[]{:S(2)}) %collective-permute-start.27) | collective-permute-done | bytes 114720 | tf_op jit(solution)/shard_map/ppermute | solution.py:32
  141.7 1.4 collective-permute-done.26
  143.1 0.2 reshape.26
  143.3 1.0 copy.3
  (53 shorter events, 0.9 us)
Async XLA Ops:
  0.0 1.5 %slice-start = ((bf16[32,8,16,128]{3,2,1,0:T(8,128)(2,1)}), bf16[32,4,16,128]{3,2,1,0:T(8,128)(2,1)S(1)}, s32[]{:S(2)}) async-start(bf16[32,8,16,128]{3,2,1,0:T(8,128)(2,1)} %param.3), calls=%async_computation | async-start | bytes 1048576 | tf_op jit(solution)/shard_map/slice | solution.py:196
  1.1 6.1 %copy-start.1 = (bf16[32,8,16,128]{3,2,1,0:T(8,128)(2,1)S(1)}, bf16[32,8,16,128]{3,2,1,0:T(8,128)(2,1)}, u32[]{:S(2)}) copy-start(bf16[32,8,16,128]{3,2,1,0:T(8,128)(2,1)} %param.2) | copy-start | bytes 3145732
  1.9 29.0 %collective-permute-start.1 = (bf16[32,8192]{1,0:T(8,128)(2,1)S(1)}, bf16[32,8192]{1,0:T(8,128)(2,1)S(1)}, u32[]{:S(2)}, u32[]{:S(2)}) collective-permute-start(bf16[32,8192]{1,0:T(8,128)(2,1)S(1)} %bitcast.44), channel_id=1, source_target_pairs={{0,12},{1,13},{2,14},{3,15},{4,8},{5,9},{6,10},{7,11},{8,4},{9,5},... | collective-permute-start | bytes 1572872 | tf_op jit(solution)/shard_map/ppermute | solution.py:32
  5.0 32.5 %collective-permute-start.9 = (bf16[32,8192]{1,0:T(8,128)(2,1)S(1)}, bf16[32,8192]{1,0:T(8,128)(2,1)S(1)}, u32[]{:S(2)}, u32[]{:S(2)}) collective-permute-start(bf16[32,8192]{1,0:T(8,128)(2,1)S(1)} %bitcast.45), channel_id=1, source_target_pairs={{0,4},{1,5},{2,6},{3,7},{4,0},{5,1},{6,2},{7,3},{8,12},{9,13},{10,... | collective-permute-start | bytes 1572872 | tf_op jit(solution)/shard_map/ppermute | solution.py:32
  5.1 24.5 %collective-permute-start = (bf16[32,8192]{1,0:T(8,128)(2,1)S(1)}, bf16[32,8192]{1,0:T(8,128)(2,1)S(1)}, u32[]{:S(2)}, u32[]{:S(2)}) collective-permute-start(bf16[32,8192]{1,0:T(8,128)(2,1)S(1)} %bitcast.40), channel_id=1, source_target_pairs={{0,4},{1,5},{2,6},{3,7},{4,0},{5,1},{6,2},{7,3},{8,12},{9,13},{10,... | collective-permute-start | bytes 1572872 | tf_op jit(solution)/shard_map/ppermute | solution.py:32
  7.0 30.9 %collective-permute-start.10 = (bf16[32,8192]{1,0:T(8,128)(2,1)S(1)}, bf16[32,8192]{1,0:T(8,128)(2,1)S(1)}, u32[]{:S(2)}, u32[]{:S(2)}) collective-permute-start(bf16[32,8192]{1,0:T(8,128)(2,1)S(1)} %bitcast.41), channel_id=1, source_target_pairs={{0,12},{1,13},{2,14},{3,15},{4,8},{5,9},{6,10},{7,11},{8,4},{9,5},... | collective-permute-start | bytes 1572872 | tf_op jit(solution)/shard_map/ppermute | solution.py:32
  7.9 6.3 %collective-permute-start.2 = (bf16[32,2048]{1,0:T(8,128)(2,1)S(1)}, bf16[32,2048]{1,0:T(8,128)(2,1)S(1)}, u32[]{:S(2)}, u32[]{:S(2)}) collective-permute-start(bf16[32,2048]{1,0:T(8,128)(2,1)S(1)} %get-tuple-element.74), channel_id=1, source_target_pairs={{0,16},{1,17},{2,18},{3,19},{4,20},{5,21},{6,22},{7,23},{8,24},{9,... | collective-permute-start | bytes 393224 | tf_op jit(solution)/shard_map/ppermute | solution.py:212
  14.3 7.3 %collective-permute-start.3 = (bf16[32,2048]{1,0:T(8,128)(2,1)S(1)}, bf16[32,2048]{1,0:T(8,128)(2,1)S(1)}, u32[]{:S(2)}, u32[]{:S(2)}) collective-permute-start(bf16[32,2048]{1,0:T(8,128)(2,1)S(1)} %get-tuple-element.73), channel_id=1, source_target_pairs={{16,0},{17,1},{18,2},{19,3},{20,4},{21,5},{22,6},{23,7},{24,8},{25... | collective-permute-start | bytes 393224 | tf_op jit(solution)/shard_map/ppermute | solution.py:212
  21.6 9.5 %collective-permute-start.7 = (bf16[32,2048]{1,0:T(8,128)(2,1)S(1)}, bf16[32,2048]{1,0:T(8,128)(2,1)S(1)}, u32[]{:S(2)}, u32[]{:S(2)}) collective-permute-start(bf16[32,2048]{1,0:T(8,128)(2,1)S(1)} %get-tuple-element.74), channel_id=1, source_target_pairs={{0,18},{1,19},{2,16},{3,17},{4,22},{5,23},{6,20},{7,21},{8,26},{9,... | collective-permute-start | bytes 393224 | tf_op jit(solution)/shard_map/ppermute | solution.py:212
  29.6 13.3 %copy-start.4 = (bf16[32,8192]{1,0:T(8,128)(2,1)}, bf16[32,8192]{1,0:T(8,128)(2,1)S(1)}, u32[]{:S(2)}) copy-start(bf16[32,8192]{1,0:T(8,128)(2,1)S(1)} %collective-permute-done.refs_4_) | copy-start | bytes 1572868
  29.6 7.8 %collective-permute-start.8 = (bf16[32,2048]{1,0:T(8,128)(2,1)S(1)}, bf16[32,2048]{1,0:T(8,128)(2,1)S(1)}, u32[]{:S(2)}, u32[]{:S(2)}) collective-permute-start(bf16[32,2048]{1,0:T(8,128)(2,1)S(1)} %get-tuple-element.73), channel_id=1, source_target_pairs={{16,2},{17,3},{18,0},{19,1},{20,6},{21,7},{22,4},{23,5},{24,10},{2... | collective-permute-start | bytes 393224 | tf_op jit(solution)/shard_map/ppermute | solution.py:212
  30.9 12.0 %copy-start.2 = (bf16[32,8192]{1,0:T(8,128)(2,1)}, bf16[32,8192]{1,0:T(8,128)(2,1)S(1)}, u32[]{:S(2)}) copy-start(bf16[32,8192]{1,0:T(8,128)(2,1)S(1)} %collective-permute-done.1.refs_13_) | copy-start | bytes 1572868
  30.9 12.0 %collective-permute-start.11 = (bf16[32,8192]{1,0:T(8,128)(2,1)S(1)}, bf16[32,8192]{1,0:T(8,128)(2,1)S(1)}, u32[]{:S(2)}, u32[]{:S(2)}) collective-permute-start(bf16[32,8192]{1,0:T(8,128)(2,1)S(1)} %bitcast.42), channel_id=1, source_target_pairs={{0,1},{1,0},{2,3},{3,2},{4,5},{5,4},{6,7},{7,6},{8,9},{9,8},{10,11... | collective-permute-start | bytes 1572872 | tf_op jit(solution)/shard_map/ppermute | solution.py:32
  31.0 27.9 %collective-permute-start.6 = (bf16[32,16384]{1,0:T(8,128)(2,1)S(1)}, bf16[32,16384]{1,0:T(8,128)(2,1)S(1)}, u32[]{:S(2)}, u32[]{:S(2)}) collective-permute-start(bf16[32,16384]{1,0:T(8,128)(2,1)S(1)} %bitcast.38), channel_id=1, source_target_pairs={{0,2},{1,3},{2,0},{3,1},{4,6},{5,7},{6,4},{7,5},{8,10},{9,11},{10,... | collective-permute-start | bytes 3145736 | tf_op jit(solution)/shard_map/ppermute | solution.py:32
  37.4 5.4 %collective-permute-start.12 = (bf16[32,8192]{1,0:T(8,128)(2,1)S(1)}, bf16[32,8192]{1,0:T(8,128)(2,1)S(1)}, u32[]{:S(2)}, u32[]{:S(2)}) collective-permute-start(bf16[32,8192]{1,0:T(8,128)(2,1)S(1)} %bitcast.46), channel_id=1, source_target_pairs={{0,1},{1,0},{2,3},{3,2},{4,5},{5,4},{6,7},{7,6},{8,9},{9,8},{10,11... | collective-permute-start | bytes 1572872 | tf_op jit(solution)/shard_map/ppermute | solution.py:32
  37.4 15.7 %copy-start.3 = (bf16[32,8192]{1,0:T(8,128)(2,1)}, bf16[32,8192]{1,0:T(8,128)(2,1)S(1)}, u32[]{:S(2)}) copy-start(bf16[32,8192]{1,0:T(8,128)(2,1)S(1)} %collective-permute-done.9.refs_5_) | copy-start | bytes 1572868
  37.5 15.7 %collective-permute-start.4 = (bf16[32,8192]{1,0:T(8,128)(2,1)S(1)}, bf16[32,8192]{1,0:T(8,128)(2,1)}, u32[]{:S(2)}, u32[]{:S(2)}) collective-permute-start(bf16[32,8192]{1,0:T(8,128)(2,1)S(1)} %collective-permute-done.refs_4_), channel_id=1, source_target_pairs={{0,12},{1,13},{2,14},{3,15},{4,8},{5,9},{6,10},{7,11},{8,4},{9,5},... | collective-permute-start | bytes 1572872 | tf_op jit(solution)/shard_map/ppermute | solution.py:32
  37.9 15.2 %copy-start.5 = (bf16[32,8192]{1,0:T(8,128)(2,1)}, bf16[32,8192]{1,0:T(8,128)(2,1)S(1)}, u32[]{:S(2)}) copy-start(bf16[32,8192]{1,0:T(8,128)(2,1)S(1)} %collective-permute-done.10.refs_12_) | copy-start | bytes 1572868
  37.9 15.2 %collective-permute-start.5 = (bf16[32,8192]{1,0:T(8,128)(2,1)S(1)}, bf16[32,8192]{1,0:T(8,128)(2,1)}, u32[]{:S(2)}, u32[]{:S(2)}) collective-permute-start(bf16[32,8192]{1,0:T(8,128)(2,1)S(1)} %collective-permute-done.1.refs_13_), channel_id=1, source_target_pairs={{0,4},{1,5},{2,6},{3,7},{4,0},{5,1},{6,2},{7,3},{8,12},{9,13},{10,... | collective-permute-start | bytes 1572872 | tf_op jit(solution)/shard_map/ppermute | solution.py:32
  42.9 16.1 %collective-permute-start.13 = (bf16[32,8192]{1,0:T(8,128)(2,1)S(1)}, bf16[32,8192]{1,0:T(8,128)(2,1)S(1)}, u32[]{:S(2)}, u32[]{:S(2)}) collective-permute-start(bf16[32,8192]{1,0:T(8,128)(2,1)S(1)} %collective-permute-done.refs_4_), channel_id=1, source_target_pairs={{0,1},{1,0},{2,3},{3,2},{4,5},{5,4},{6,7},{7,6},{8,9},{9,8},{10,11... | collective-permute-start | bytes 1572872 | tf_op jit(solution)/shard_map/ppermute | solution.py:32
  42.9 16.1 %copy-start.6 = (bf16[32,8192]{1,0:T(8,128)(2,1)}, bf16[32,8192]{1,0:T(8,128)(2,1)S(1)}, u32[]{:S(2)}) copy-start(bf16[32,8192]{1,0:T(8,128)(2,1)S(1)} %collective-permute-done.12.refs_3_) | copy-start | bytes 1572868
  42.9 16.1 %collective-permute-start.14 = (bf16[32,8192]{1,0:T(8,128)(2,1)S(1)}, bf16[32,8192]{1,0:T(8,128)(2,1)S(1)}, u32[]{:S(2)}, u32[]{:S(2)}) collective-permute-start(bf16[32,8192]{1,0:T(8,128)(2,1)S(1)} %collective-permute-done.1.refs_13_), channel_id=1, source_target_pairs={{0,1},{1,0},{2,3},{3,2},{4,5},{5,4},{6,7},{7,6},{8,9},{9,8},{10,11... | collective-permute-start | bytes 1572872 | tf_op jit(solution)/shard_map/ppermute | solution.py:32
  53.1 5.9 %collective-permute-start.15 = (bf16[32,8192]{1,0:T(8,128)(2,1)S(1)}, bf16[32,8192]{1,0:T(8,128)(2,1)S(1)}, u32[]{:S(2)}, u32[]{:S(2)}) collective-permute-start(bf16[32,8192]{1,0:T(8,128)(2,1)S(1)} %collective-permute-done.9.refs_5_), channel_id=1, source_target_pairs={{0,1},{1,0},{2,3},{3,2},{4,5},{5,4},{6,7},{7,6},{8,9},{9,8},{10,11... | collective-permute-start | bytes 1572872 | tf_op jit(solution)/shard_map/ppermute | solution.py:32
  53.1 5.9 %collective-permute-start.16 = (bf16[32,8192]{1,0:T(8,128)(2,1)S(1)}, bf16[32,8192]{1,0:T(8,128)(2,1)S(1)}, u32[]{:S(2)}, u32[]{:S(2)}) collective-permute-start(bf16[32,8192]{1,0:T(8,128)(2,1)S(1)} %collective-permute-done.10.refs_12_), channel_id=1, source_target_pairs={{0,1},{1,0},{2,3},{3,2},{4,5},{5,4},{6,7},{7,6},{8,9},{9,8},{10,11... | collective-permute-start | bytes 1572872 | tf_op jit(solution)/shard_map/ppermute | solution.py:32
  58.9 0.8 copy-start.7
  59.0 1.0 copy-start.8
  59.0 1.1 copy-start.9
  59.0 1.3 copy-start.10
  59.0 6.0 %collective-permute-start.17 = (bf16[32,8192]{1,0:T(8,128)(2,1)}, bf16[32,8192]{1,0:T(8,128)(2,1)S(1)}, u32[]{:S(2)}, u32[]{:S(2)}) collective-permute-start(bf16[32,8192]{1,0:T(8,128)(2,1)} %collective-permute-done.4.refs_8_), channel_id=1, source_target_pairs={{0,1},{1,0},{2,3},{3,2},{4,5},{5,4},{6,7},{7,6},{8,9},{9,8},{10,11... | collective-permute-start | bytes 1572872 | tf_op jit(solution)/shard_map/ppermute | solution.py:32
  59.8 5.2 %collective-permute-start.18 = (bf16[32,8192]{1,0:T(8,128)(2,1)}, bf16[32,8192]{1,0:T(8,128)(2,1)}, u32[]{:S(2)}, u32[]{:S(2)}) collective-permute-start(bf16[32,8192]{1,0:T(8,128)(2,1)} %collective-permute-done.5.refs_9_), channel_id=1, source_target_pairs={{0,1},{1,0},{2,3},{3,2},{4,5},{5,4},{6,7},{7,6},{8,9},{9,8},{10,11... | collective-permute-start | bytes 1572872 | tf_op jit(solution)/shard_map/ppermute | solution.py:32
  65.0 0.8 copy-start.11
  93.2 24.5 %copy-start = (f32[8,2,32,896]{3,2,1,0:T(8,128)S(1)}, f32[8,2,32,896]{3,2,1,0:T(8,128)}, u32[]{:S(2)}) copy-start(f32[8,2,32,896]{3,2,1,0:T(8,128)} %shard_map.30) | copy-start | bytes 5505028
  94.5 10.8 %collective-permute-start.20 = (f32[2,32,896]{2,1,0:T(8,128)S(1)}, f32[2,32,896]{2,1,0:T(8,128)S(1)}, u32[]{:S(2)}, u32[]{:S(2)}) collective-permute-start(f32[2,32,896]{2,1,0:T(8,128)S(1)} %get-tuple-element.71), channel_id=1, source_target_pairs={{0,112},{1,113},{2,114},{3,115},{4,116},{5,117},{6,118},{7,119},{8... | collective-permute-start | bytes 688136 | tf_op jit(solution)/shard_map/ppermute | solution.py:32
  100.2 8.5 %collective-permute-start.19 = (f32[2,32,896]{2,1,0:T(8,128)S(1)}, f32[2,32,896]{2,1,0:T(8,128)S(1)}, u32[]{:S(2)}, u32[]{:S(2)}) collective-permute-start(f32[2,32,896]{2,1,0:T(8,128)S(1)} %get-tuple-element.72), channel_id=1, source_target_pairs={{0,16},{1,17},{2,18},{3,19},{4,20},{5,21},{6,22},{7,23},{8,24},{9,... | collective-permute-start | bytes 688136 | tf_op jit(solution)/shard_map/ppermute | solution.py:32
  109.8 6.5 %collective-permute-start.22 = (f32[2,32,896]{2,1,0:T(8,128)S(1)}, f32[2,32,896]{2,1,0:T(8,128)S(1)}, u32[]{:S(2)}, u32[]{:S(2)}) collective-permute-start(f32[2,32,896]{2,1,0:T(8,128)S(1)} %get-tuple-element.62), channel_id=1, source_target_pairs={{0,112},{1,113},{2,114},{3,115},{4,116},{5,117},{6,118},{7,119},{8... | collective-permute-start | bytes 688136 | tf_op jit(solution)/shard_map/ppermute | solution.py:32
  110.4 7.3 %collective-permute-start.21 = (f32[2,32,896]{2,1,0:T(8,128)S(1)}, f32[2,32,896]{2,1,0:T(8,128)S(1)}, u32[]{:S(2)}, u32[]{:S(2)}) collective-permute-start(f32[2,32,896]{2,1,0:T(8,128)S(1)} %get-tuple-element.61), channel_id=1, source_target_pairs={{0,16},{1,17},{2,18},{3,19},{4,20},{5,21},{6,22},{7,23},{8,24},{9,... | collective-permute-start | bytes 688136 | tf_op jit(solution)/shard_map/ppermute | solution.py:32
  117.8 7.3 %collective-permute-start.23 = (f32[2,32,896]{2,1,0:T(8,128)S(1)}, f32[2,32,896]{2,1,0:T(8,128)S(1)}, u32[]{:S(2)}, u32[]{:S(2)}) collective-permute-start(f32[2,32,896]{2,1,0:T(8,128)S(1)} %get-tuple-element.63), channel_id=1, source_target_pairs={{0,16},{1,17},{2,18},{3,19},{4,20},{5,21},{6,22},{7,23},{8,24},{9,... | collective-permute-start | bytes 688136 | tf_op jit(solution)/shard_map/ppermute | solution.py:32
  125.1 7.3 %collective-permute-start.24 = (f32[2,32,896]{2,1,0:T(8,128)S(1)}, f32[2,32,896]{2,1,0:T(8,128)S(1)}, u32[]{:S(2)}, u32[]{:S(2)}) collective-permute-start(f32[2,32,896]{2,1,0:T(8,128)S(1)} %bitcast_add_fusion.1), channel_id=1, source_target_pairs={{0,16},{1,17},{2,18},{3,19},{4,20},{5,21},{6,22},{7,23},{8,24},{9,... | collective-permute-start | bytes 688136 | tf_op jit(solution)/shard_map/ppermute | solution.py:32
  125.2 7.2 %collective-permute-start.25 = (f32[2,32,896]{2,1,0:T(8,128)S(1)}, f32[2,32,896]{2,1,0:T(8,128)S(1)}, u32[]{:S(2)}, u32[]{:S(2)}) collective-permute-start(f32[2,32,896]{2,1,0:T(8,128)S(1)} %get-tuple-element.66), channel_id=1, source_target_pairs={{0,112},{1,113},{2,114},{3,115},{4,116},{5,117},{6,118},{7,119},{8... | collective-permute-start | bytes 688136 | tf_op jit(solution)/shard_map/ppermute | solution.py:32
  132.5 9.1 %collective-permute-start.27 = (f32[32,896]{1,0:T(8,128)S(1)}, f32[32,896]{1,0:T(8,128)S(1)}, u32[]{:S(2)}, u32[]{:S(2)}) collective-permute-start(f32[32,896]{1,0:T(8,128)S(1)} %get-tuple-element.76), channel_id=1, source_target_pairs={{0,128},{1,129},{2,160},{3,161},{4,132},{5,133},{6,164},{7,165},{8... | collective-permute-start | bytes 344072 | tf_op jit(solution)/shard_map/ppermute | solution.py:32
  134.6 8.5 %collective-permute-start.26 = (f32[32,896]{1,0:T(8,128)S(1)}, f32[32,896]{1,0:T(8,128)S(1)}, u32[]{:S(2)}, u32[]{:S(2)}) collective-permute-start(f32[32,896]{1,0:T(8,128)S(1)} %get-tuple-element.75), channel_id=1, source_target_pairs={{0,0},{1,1},{2,32},{3,33},{4,4},{5,5},{6,36},{7,37},{8,8},{9,9},{1... | collective-permute-start | bytes 344072 | tf_op jit(solution)/shard_map/ppermute | solution.py:32
where the time goes:
time: 146 us; the launch traced here: 144 us
  waiting for transfers between devices  61.8 us (42%)
  starting transfers between devices  37.2 us (25%)
  Pallas kernels  36.7 us (25%)
  local copies, waits for them, and re-layouts  6.93 us (5%)
    ppermute x24, waiting for transfers between devices, send(): return lax.ppermute(value, AXES, pairs)  47.5 us
    pallas_call x1, Pallas kernels, product(): pl.pallas_call(functools.partial(product_body, cuts, slabs, size_z), grid...  27.4 us
    ppermute x24, starting transfers between devices, send(): return lax.ppermute(value, AXES, pairs)  27 us
    ppermute x4, waiting for transfers between devices, move(): return lax.ppermute(value, AXES, pairs)  14.3 us
    ppermute x4, starting transfers between devices, move(): return lax.ppermute(value, AXES, pairs)  10.3 us
    pallas_call x2, Pallas kernels, spread(): pl.pallas_call(functools.partial(spread_body, size_z, slabs, lanes), grid...  9.34 us
    unnamed x27, local copies, waits for them, and re-layouts  3.32 us
  transfers between devices with their start and end apart: 28, of which 14 were waited for; matrix products, arithmetic and copies ran while one was open for 1% of the time, Pallas kernels for 6%

commit v1 on v0

--- a/solution.py
+++ b/solution.py
@@ -79,44 +79,65 @@
     )(cells, edges)
 
 
-def product_body(cuts, slabs, size_z, *refs):
+def product_body(cuts, slabs, size_z, terms, field_count, *refs):
     count = len(cuts)
     refs = list(refs)
     blocks = [[refs.pop(0) for _ in range(cut)] for cut in cuts]
-    own, near, out_ref, held, total, sems = refs
+    fields = [refs.pop(0) for _ in range(field_count)]
+    sems = refs.pop()
+    held = refs.pop()
+    if field_count > 1:
+        early, out_ref, *totals = refs
+    else:
+        totals = refs
     x = pl.program_id(0)
     lanes = held.shape[1] // slabs
     rows = held.shape[0] // count
-    tall = count * rows
+
+    def arrivals(at):
+        copies = []
+        for i, parts in enumerate(blocks):
+            part, inner = divmod(at, slabs // len(parts))
+            copies.append(
+                pltpu.make_async_copy(
+                    parts[part].at[:, pl.ds(inner * lanes, lanes)],
+                    held.at[pl.ds(i * rows, rows), pl.ds(at * lanes, lanes)],
+                    sems.at[i, at],
+                )
+            )
+        return copies
 
     @pl.when(x == 0)
     def _():
-        copies = []
-        for i, parts in enumerate(blocks):
-            width = held.shape[1] // len(parts)
-            for j, part in enumerate(parts):
-                to = held.at[pl.ds(i * rows, rows), pl.ds(j * width, width)]
-                copies.append(pltpu.make_async_copy(part, to, sems.at[len(copies)]))
-        for copy in copies:
-            copy.start()
-        total[...] = jnp.zeros_like(total)
-        for copy in copies:
+        for at in range(slabs):
+            for copy in arrivals(at):
+                copy.start()
+        for total in totals:
+            total[...] = jnp.zeros_like(total)
+
+    def arrived(at):
+        for copy in arrivals(at):
             copy.wait()
 
+    for at in range(slabs):
+        pl.when(x == at)(functools.partial(arrived, at))
+
     def add(first, last):
-        left = jnp.concatenate(
-            [
-                held[:, pl.ds(pl.multiple_of((x - a) * lanes, lanes), lanes)]
-                for a in range(first, last)
-            ],
-            axis=0,
-        )
-        for b in range(3):
-            at = slice(b * size_z, b * size_z + lanes)
-            total[b, first * tall : last * tall] += jnp.dot(
-                left,
-                jnp.concatenate([own[0, at, :], near[0, at, :]], axis=1),
-                preferred_element_type=jnp.float32,
+        for total, (low, high, sides) in zip(totals, terms):
+            tall = (high - low) * rows
+            left = jnp.concatenate(
+                [
+                    held[
+                        low * rows : high * rows,
+                        pl.ds(pl.multiple_of((x - a) * lanes, lanes), lanes),
+                    ]
+                    for a in range(first, last)
+                ],
+                axis=0,
+            )
+            right = [fields[f][0, b * size_z : b * size_z + lanes, :] for f, b in sides]
+            total[first * tall : last * tall] += jnp.dot(
+                left, jnp.concatenate(right, axis=1), preferred_element_type=jnp.float32
             )
 
     for first, last, chosen in (
@@ -128,43 +149,67 @@
     ):
         pl.when(chosen)(functools.partial(add, first, last))
 
+    if field_count == 1:
+        return
+
     @pl.when(x == slabs + 1)
     def _():
-        for block in range(count):
+        late, beside, third = totals
+        for i, block in enumerate((0, 1, 2, 3, 6, 7, 4, 5)):
             for n in range(2):
                 for a in range(3):
                     for b in range(3):
-                        at = a * tall + block * rows
+                        if b == 2:
+                            source, at, column = third, a * 8 + i, n
+                        elif n == 1:
+                            source, at, column = beside, a * 8 + i, b
+                        elif i < 6:
+                            source, at, column = early, a * 6 + i, b
+                        else:
+                            source, at, column = late, a * 2 + i - 6, b
                         to = (3 * a + b) * 96
-                        out_ref[block, n, :, to : to + 96] = total[
-                            b, at : at + rows, n * 128 : n * 128 + 96
+                        out_ref[block, n, :, to : to + 96] = source[
+                            at * rows : (at + 1) * rows, column * 128 : column * 128 + 96
                         ]
                 out_ref[block, n, :, 864:] = jnp.zeros((rows, 32), jnp.float32)
 
 
-def product(blocks, own, near, size_z):
+def product(blocks, fields, early, size_z):
     count = len(blocks)
     rows = blocks[0][0].shape[0]
-    slabs = own.shape[0] - 2
-    cells = slabs * (own.shape[1] - 2 * size_z)
+    shape = fields[0].shape
+    slabs = shape[0] - 2
+    cells = slabs * (shape[1] - 2 * size_z)
     cuts = tuple(len(parts) for parts in blocks)
-    field = pl.BlockSpec((1,) + own.shape[1:], lambda x: (x, 0, 0))
+    field = pl.BlockSpec((1,) + shape[1:], lambda x: (x, 0, 0))
+    whole = pl.BlockSpec((3 * 6 * rows, 256), lambda x: (0, 0))
+    in_specs = [pl.BlockSpec(memory_space=pl.ANY)] * sum(cuts) + [field] * len(fields)
+    scratch = []
+    if early is None:
+        terms = ((0, 6, ((0, 0), (0, 1))),)
+        out_specs, out_shape = whole, jax.ShapeDtypeStruct((3 * 6 * rows, 256), jnp.float32)
+    else:
+        terms = ((6, 8, ((0, 0), (0, 1))), (0, 8, ((1, 0), (1, 1))), (0, 8, ((0, 2), (1, 2))))
+        in_specs.append(whole)
+        out_specs = pl.BlockSpec((count, 2, rows, 896), lambda x: (0, 0, 0, 0))
+        out_shape = jax.ShapeDtypeStruct((count, 2, rows, 896), jnp.float32)
+        scratch = [pltpu.VMEM((3 * (h - w) * rows, 256), jnp.float32) for w, h, _ in terms]
     return pl.pallas_call(
-        functools.partial(product_body, cuts, slabs, size_z),
+        functools.partial(product_body, cuts, slabs, size_z, terms, len(fields)),
         grid=(slabs + 2,),
-        in_specs=[pl.BlockSpec(memory_space=pl.ANY)] * sum(cuts) + [field, field],
-        out_specs=pl.BlockSpec((count, 2, rows, 896), lambda x: (0, 0, 0, 0)),
-        out_shape=jax.ShapeDtypeStruct((count, 2, rows, 896), jnp.float32),
-        scratch_shapes=[
-            pltpu.VMEM((count * rows, cells), own.dtype),
-            pltpu.VMEM((3, 3 * count * rows, 2 * own.shape[2]), jnp.float32),
-            pltpu.SemaphoreType.DMA((sum(cuts),)),
+        in_specs=in_specs,
+        out_specs=out_specs,
+        out_shape=out_shape,
+        scratch_shapes=scratch
+        + [
+            pltpu.VMEM((count * rows, cells), fields[0].dtype),
+            pltpu.SemaphoreType.DMA((count, slabs)),
         ],
         compiler_params=pltpu.CompilerParams(vmem_limit_bytes=VMEM),
         cost_estimate=pl.CostEstimate(
-            flops=count * 3 * 10**9, bytes_accessed=16 * 2**20, transcendentals=0
+            flops=len(terms) * 6 * 10**9, bytes_accessed=16 * 2**20, transcendentals=0
         ),
-    )(*[part for parts in blocks for part in parts], own, near)
+    )(*[part for parts in blocks for part in parts], *fields, *([] if early is None else [early]))
 
 
 def ring_sum(piece):
@@ -220,23 +265,24 @@
     next_one, last_two, next_two, last_one, own = lax.optimization_barrier(
         (next_one, last_two, next_two, last_one, own)
     )
-    mates = [shift(v, k=1) for v in (one, two, next_one, last_two, next_two, last_one)]
-    far_one, far_two, acts_near, near_ends, own, mates = lax.optimization_barrier(
-        (far_one, far_two, acts_near, near_ends, own, mates)
-    )
-    far_mate = shift(far_one, k=1), shift(far_two, k=1)
-    near = spread(acts_near, jnp.concatenate(near_ends, axis=1), size_z, lanes)
+    mates = [
+        send(v, lambda d: dict(d, k=d["k"] ^ 1))
+        for v in (one, two, next_one, last_two, next_two, last_one)
+    ]
     blocks = (
         (one, two),
         (mates[0], mates[1]),
         (next_one, next_two),
         (mates[2], mates[4]),
-        (far_one, far_two),
-        far_mate,
         (last_one, last_two),
         (mates[5], mates[3]),
     )
-    parts = product(blocks, own, near, size_z)
+    early = product(blocks, (own,), None, size_z)
+    early, acts_near, near_ends = lax.optimization_barrier((early, acts_near, near_ends))
+    near = spread(acts_near, jnp.concatenate(near_ends, axis=1), size_z, lanes)
+    far_one, far_two, near = lax.optimization_barrier((far_one, far_two, near))
+    far_mate = shift(far_one, k=1), shift(far_two, k=1)
+    parts = product(blocks + ((far_one, far_two), far_mate), (own, near), early, size_z)
 
     def piece(step):
         to = lax.rem(z + step + 8, 8)

time: 146 us -> 144 us (0.986)
  waiting for transfers between devices: 61.8 us -> 50.4 us
  Pallas kernels: 36.7 us -> 43.5 us
  starting transfers between devices: 37.2 us -> 40.2 us
    ppermute x4, waiting for transfers between devices: 14.3 us -> 3.75 us  [move(): return lax.ppermute(value, AXES, pairs)]
    pallas_call x1 -> x2, Pallas kernels: 27.4 us -> 34.2 us  [product(): pl.pallas_call(functools.partial(product_body, cuts, slabs, size_z, terms...]
    ppermute x24, starting transfers between devices: 27 us -> 29.4 us  [send(): return lax.ppermute(value, AXES, pairs)]
    unnamed x27 -> x29, local copies, waits for them, and re-layouts: 3.32 us -> 2.71 us
  transfers between devices with their start and end apart: 28 -> 28, of which waited for: 14 -> 17; matrix products, arithmetic and copies ran while one was open for 1% -> 1% of each run, Pallas kernels for 6% -> 15%
where the time goes in v1:
time: 144 us; the launch traced here: 142 us
  waiting for transfers between devices  50.4 us (35%)
  Pallas kernels  43.5 us (30%)
  starting transfers between devices  40.2 us (28%)
  local copies, waits for them, and re-layouts  6.32 us (4%)
    ppermute x24, waiting for transfers between devices, send(): return lax.ppermute(value, AXES, pairs)  46.7 us
    pallas_call x2, Pallas kernels, product(): pl.pallas_call(functools.partial(product_body, cuts, slabs, size_z, terms...  34.2 us
    ppermute x24, starting transfers between devices, send(): return lax.ppermute(value, AXES, pairs)  29.4 us
    ppermute x4, starting transfers between devices, move(): return lax.ppermute(value, AXES, pairs)  10.8 us
    pallas_call x2, Pallas kernels, spread(): pl.pallas_call(functools.partial(spread_body, size_z, slabs, lanes), grid...  9.32 us
    ppermute x4, waiting for transfers between devices, move(): return lax.ppermute(value, AXES, pairs)  3.75 us
  transfers between devices with their start and end apart: 28, of which 17 were waited for; matrix products, arithmetic and copies ran while one was open for 1% of the time, Pallas kernels for 15%

profile of v1, /device:TPU:2, one launch (start us, length us, event | category | flops | bytes accessed | tf_op | source)
XLA Modules:
  0.0 142.1 jit_solution(15106339701634298781)
XLA Ops:
  0.0 1.1 slice.17
  1.2 0.3 copy.12
  1.5 1.7 %collective-permute-start.2 = (bf16[32,8192]{1,0:T(8,128)(2,1)S(1)}, bf16[32,8192]{1,0:T(8,128)(2,1)S(1)}, u32[]{:S(2)}, u32[]{:S(2)}) collective-permute-start(bf16[32,8192]{1,0:T(8,128)(2,1)S(1)} %bitcast.40), channel_id=1, source_target_pairs={{0,4},{1,5},{2,6},{3,7},{4,0},{5,1},{6,2},{7,3},{8,12},{9,13},{10,... | collective-permute-start | bytes 1572872 | tf_op jit(solution)/shard_map/ppermute | solution.py:32
  3.2 0.3 copy.11
  3.5 2.3 %collective-permute-start.3 = (bf16[32,8192]{1,0:T(8,128)(2,1)S(1)}, bf16[32,8192]{1,0:T(8,128)(2,1)S(1)}, u32[]{:S(2)}, u32[]{:S(2)}) collective-permute-start(bf16[32,8192]{1,0:T(8,128)(2,1)S(1)} %bitcast.45), channel_id=1, source_target_pairs={{0,12},{1,13},{2,14},{3,15},{4,8},{5,9},{6,10},{7,11},{8,4},{9,5},... | collective-permute-start | bytes 1572872 | tf_op jit(solution)/shard_map/ppermute | solution.py:32
  5.8 0.7 copy.10
  6.5 3.8 %collective-permute-start.4 = (bf16[32,2048]{1,0:T(8,128)(2,1)S(1)}, bf16[32,2048]{1,0:T(8,128)(2,1)S(1)}, u32[]{:S(2)}, u32[]{:S(2)}) collective-permute-start(bf16[32,2048]{1,0:T(8,128)(2,1)S(1)} %get-tuple-element.64), channel_id=1, source_target_pairs={{0,16},{1,17},{2,18},{3,19},{4,20},{5,21},{6,22},{7,23},{8,24},{9,... | collective-permute-start | bytes 393224 | tf_op jit(solution)/shard_map/ppermute | solution.py:257
  10.3 1.3 collective-permute-start.5
  11.6 0.8 collective-permute-start.6
  12.4 0.4 collective-permute-done.4
  12.8 1.1 collective-permute-start.7
  13.9 3.3 %collective-permute-done.5 = bf16[32,2048]{1,0:T(8,128)(2,1)S(1)} collective-permute-done((bf16[32,2048]{1,0:T(8,128)(2,1)S(1)}, bf16[32,2048]{1,0:T(8,128)(2,1)S(1)}, u32[]{:S(2)}, u32[]{:S(2)}) %collective-permute-start.5) | collective-permute-done | bytes 131104 | tf_op jit(solution)/shard_map/ppermute | solution.py:257
  17.2 0.5 collective-permute-start.1
  17.7 1.9 %collective-permute-done.3.refs_9_ = bf16[32,8192]{1,0:T(8,128)(2,1)S(1)} collective-permute-done((bf16[32,8192]{1,0:T(8,128)(2,1)S(1)}, bf16[32,8192]{1,0:T(8,128)(2,1)S(1)}, u32[]{:S(2)}, u32[]{:S(2)}) %collective-permute-start.3) | collective-permute-done | bytes 524320 | tf_op jit(solution)/shard_map/ppermute | solution.py:32
  19.6 4.7 %shard_map.28.refs_12_.refs_16_ = bf16[10,2304,128]{2,1,0:T(8,128)(2,1)} custom-call(bf16[32,16384]{1,0:T(8,128)(2,1)S(1)} %bitcast.38, bf16[32,4096]{1,0:T(8,128)(2,1)S(1)} %pad_maximum_fusion.edge), custom_call_target="tpu_custom_call" | custom-call | flops 10485760 | bytes 10485760 | tf_op jit(solution)/shard_map/pallas_call | solution.py:66
  24.3 2.2 %collective-permute-done.6.refs_5_ = bf16[32,8192]{1,0:T(8,128)(2,1)S(1)} collective-permute-done((bf16[32,8192]{1,0:T(8,128)(2,1)S(1)}, bf16[32,8192]{1,0:T(8,128)(2,1)S(1)}, u32[]{:S(2)}, u32[]{:S(2)}) %collective-permute-start.6) | collective-permute-done | bytes 524320 | tf_op jit(solution)/shard_map/ppermute | solution.py:32
  26.5 2.9 %collective-permute-done.7.refs_8_ = bf16[32,8192]{1,0:T(8,128)(2,1)S(1)} collective-permute-done((bf16[32,8192]{1,0:T(8,128)(2,1)S(1)}, bf16[32,8192]{1,0:T(8,128)(2,1)S(1)}, u32[]{:S(2)}, u32[]{:S(2)}) %collective-permute-start.7) | collective-permute-done | bytes 524320 | tf_op jit(solution)/shard_map/ppermute | solution.py:32
  29.4 0.5 collective-permute-start.9
  30.0 0.5 collective-permute-start.11
  30.5 0.5 collective-permute-start.14
  31.4 4.4 %collective-permute-start.15 = (bf16[32,2048]{1,0:T(8,128)(2,1)S(1)}, bf16[32,2048]{1,0:T(8,128)(2,1)S(1)}, u32[]{:S(2)}, u32[]{:S(2)}) collective-permute-start(bf16[32,2048]{1,0:T(8,128)(2,1)S(1)} %get-tuple-element.64), channel_id=1, source_target_pairs={{0,18},{1,19},{2,16},{3,17},{4,22},{5,23},{6,20},{7,21},{8,26},{9,... | collective-permute-start | bytes 393224 | tf_op jit(solution)/shard_map/ppermute | solution.py:257
  35.8 1.3 collective-permute-start.16
  37.1 2.3 %collective-permute-start.12 = (bf16[32,8192]{1,0:T(8,128)(2,1)S(1)}, bf16[32,8192]{1,0:T(8,128)(2,1)}, u32[]{:S(2)}, u32[]{:S(2)}) collective-permute-start(bf16[32,8192]{1,0:T(8,128)(2,1)S(1)} %collective-permute-done.2.refs_4_), channel_id=1, source_target_pairs={{0,12},{1,13},{2,14},{3,15},{4,8},{5,9},{6,10},{7,11},{8,4},{9,5},... | collective-permute-start | bytes 1572872 | tf_op jit(solution)/shard_map/ppermute | solution.py:32
  39.7 0.5 copy-done.10
  40.2 12.1 %shard_map.29.refs_18_ = f32[576,256]{1,0:T(8,128)} custom-call(bf16[32,8192]{1,0:T(8,128)(2,1)S(1)} %bitcast.43, bf16[32,8192]{1,0:T(8,128)(2,1)S(1)} %bitcast.48, bf16[32,8192]{1,0:T(8,128)(2,1)S(1)} %collective-permute-done.refs_2_, bf16[32,8192]{1,0:T(8,128)(2,1)} %copy-done.6, bf16[32,8192]{1,0:T(8,128)(2,1)} %copy-done.2, bf16[32,8192]{1,0:T(8,128)(2,1)} %copy-done.4, ...), custom_call_target="tpu_custom_call" | custom-call | flops 6000000000 | bytes 16777216 | tf_op jit(solution)/shard_map/pallas_call | solution.py:197
  52.4 6.1 %collective-permute-done.14.middle = bf16[32,16384]{1,0:T(8,128)(2,1)S(1)} collective-permute-done((bf16[32,16384]{1,0:T(8,128)(2,1)S(1)}, bf16[32,16384]{1,0:T(8,128)(2,1)S(1)}, u32[]{:S(2)}, u32[]{:S(2)}) %collective-permute-start.14) | collective-permute-done | bytes 1048608 | tf_op jit(solution)/shard_map/ppermute | solution.py:32
  58.5 4.6 %shard_map.30.refs_17_ = bf16[10,2304,128]{2,1,0:T(8,128)(2,1)} custom-call(bf16[32,16384]{1,0:T(8,128)(2,1)S(1)} %collective-permute-done.14.middle, bf16[32,4096]{1,0:T(8,128)(2,1)S(1)} %pad_maximum_fusion.1.edge), custom_call_target="tpu_custom_call" | custom-call | flops 10485760 | bytes 10485760 | tf_op jit(solution)/shard_map/pallas_call | solution.py:66
  63.1 0.5 collective-permute-start.18
  63.6 1.6 %collective-permute-done.17.refs_14_ = bf16[32,8192]{1,0:T(8,128)(2,1)S(1)} collective-permute-done((bf16[32,8192]{1,0:T(8,128)(2,1)}, bf16[32,8192]{1,0:T(8,128)(2,1)S(1)}, u32[]{:S(2)}, u32[]{:S(2)}) %collective-permute-start.17) | collective-permute-done | bytes 524320 | tf_op jit(solution)/shard_map/ppermute | solution.py:32
  65.2 0.7 collective-permute-done.18.refs_15_
  66.0 0.8 copy-done.12
  66.8 22.0 %shard_map.31 = f32[8,2,32,896]{3,2,1,0:T(8,128)} custom-call(bf16[32,8192]{1,0:T(8,128)(2,1)S(1)} %bitcast.44, bf16[32,8192]{1,0:T(8,128)(2,1)S(1)} %bitcast.49, bf16[32,8192]{1,0:T(8,128)(2,1)S(1)} %collective-permute-done.refs_2_, bf16[32,8192]{1,0:T(8,128)(2,1)} %copy-done.6, bf16[32,8192]{1,0:T(8,128)(2,1)} %copy-done.2, bf16[32,8192]{1,0:T(8,128)(2,1)} %copy-done.4, ...), custom_call_target="tpu_custom_call" | custom-call | flops 17999998976 | bytes 16777216 | tf_op jit(solution)/shard_map/pallas_call | solution.py:197
  88.9 1.2 dynamic-slice_bitcast_fusion
  90.1 5.9 %collective-permute-start.20 = (f32[2,32,896]{2,1,0:T(8,128)S(1)}, f32[2,32,896]{2,1,0:T(8,128)S(1)}, u32[]{:S(2)}, u32[]{:S(2)}) collective-permute-start(f32[2,32,896]{2,1,0:T(8,128)S(1)} %get-tuple-element.61), channel_id=1, source_target_pairs={{0,112},{1,113},{2,114},{3,115},{4,116},{5,117},{6,118},{7,119},{8... | collective-permute-start | bytes 688136 | tf_op jit(solution)/shard_map/ppermute | solution.py:32
  96.0 5.2 %collective-permute-done.20 = f32[2,32,896]{2,1,0:T(8,128)S(1)} collective-permute-done((f32[2,32,896]{2,1,0:T(8,128)S(1)}, f32[2,32,896]{2,1,0:T(8,128)S(1)}, u32[]{:S(2)}, u32[]{:S(2)}) %collective-permute-start.20) | collective-permute-done | bytes 229408 | tf_op jit(solution)/shard_map/ppermute | solution.py:32
  101.2 4.3 %collective-permute-done.19 = f32[2,32,896]{2,1,0:T(8,128)S(1)} collective-permute-done((f32[2,32,896]{2,1,0:T(8,128)S(1)}, f32[2,32,896]{2,1,0:T(8,128)S(1)}, u32[]{:S(2)}, u32[]{:S(2)}) %collective-permute-start.19) | collective-permute-done | bytes 229408 | tf_op jit(solution)/shard_map/ppermute | solution.py:32
  105.5 1.1 bitcast_add_fusion.4
  106.6 1.8 %collective-permute-start.22 = (f32[2,32,896]{2,1,0:T(8,128)S(1)}, f32[2,32,896]{2,1,0:T(8,128)S(1)}, u32[]{:S(2)}, u32[]{:S(2)}) collective-permute-start(f32[2,32,896]{2,1,0:T(8,128)S(1)} %get-tuple-element.52), channel_id=1, source_target_pairs={{0,112},{1,113},{2,114},{3,115},{4,116},{5,117},{6,118},{7,119},{8... | collective-permute-start | bytes 688136 | tf_op jit(solution)/shard_map/ppermute | solution.py:32
  108.7 4.8 %collective-permute-done.22 = f32[2,32,896]{2,1,0:T(8,128)S(1)} collective-permute-done((f32[2,32,896]{2,1,0:T(8,128)S(1)}, f32[2,32,896]{2,1,0:T(8,128)S(1)}, u32[]{:S(2)}, u32[]{:S(2)}) %collective-permute-start.22) | collective-permute-done | bytes 229408 | tf_op jit(solution)/shard_map/ppermute | solution.py:32
  113.4 2.4 %collective-permute-done.21 = f32[2,32,896]{2,1,0:T(8,128)S(1)} collective-permute-done((f32[2,32,896]{2,1,0:T(8,128)S(1)}, f32[2,32,896]{2,1,0:T(8,128)S(1)}, u32[]{:S(2)}, u32[]{:S(2)}) %collective-permute-start.21) | collective-permute-done | bytes 229408 | tf_op jit(solution)/shard_map/ppermute | solution.py:32
  116.1 7.1 %collective-permute-done.23 = f32[2,32,896]{2,1,0:T(8,128)S(1)} collective-permute-done((f32[2,32,896]{2,1,0:T(8,128)S(1)}, f32[2,32,896]{2,1,0:T(8,128)S(1)}, u32[]{:S(2)}, u32[]{:S(2)}) %collective-permute-start.23) | collective-permute-done | bytes 229408 | tf_op jit(solution)/shard_map/ppermute | solution.py:32
  123.3 3.2 %collective-permute-start.25 = (f32[2,32,896]{2,1,0:T(8,128)S(1)}, f32[2,32,896]{2,1,0:T(8,128)S(1)}, u32[]{:S(2)}, u32[]{:S(2)}) collective-permute-start(f32[2,32,896]{2,1,0:T(8,128)S(1)} %get-tuple-element.56), channel_id=1, source_target_pairs={{0,112},{1,113},{2,114},{3,115},{4,116},{5,117},{6,118},{7,119},{8... | collective-permute-start | bytes 688136 | tf_op jit(solution)/shard_map/ppermute | solution.py:32
  126.5 4.0 %collective-permute-done.24 = f32[2,32,896]{2,1,0:T(8,128)S(1)} collective-permute-done((f32[2,32,896]{2,1,0:T(8,128)S(1)}, f32[2,32,896]{2,1,0:T(8,128)S(1)}, u32[]{:S(2)}, u32[]{:S(2)}) %collective-permute-start.24) | collective-permute-done | bytes 229408 | tf_op jit(solution)/shard_map/ppermute | solution.py:32
  130.6 1.7 %collective-permute-start.27 = (f32[32,896]{1,0:T(8,128)S(1)}, f32[32,896]{1,0:T(8,128)S(1)}, u32[]{:S(2)}, u32[]{:S(2)}) collective-permute-start(f32[32,896]{1,0:T(8,128)S(1)} %get-tuple-element.66), channel_id=1, source_target_pairs={{0,128},{1,129},{2,160},{3,161},{4,132},{5,133},{6,164},{7,165},{8... | collective-permute-start | bytes 344072 | tf_op jit(solution)/shard_map/ppermute | solution.py:32
  132.3 5.4 %collective-permute-start.26 = (f32[32,896]{1,0:T(8,128)S(1)}, f32[32,896]{1,0:T(8,128)S(1)}, u32[]{:S(2)}, u32[]{:S(2)}) collective-permute-start(f32[32,896]{1,0:T(8,128)S(1)} %get-tuple-element.65), channel_id=1, source_target_pairs={{0,0},{1,1},{2,32},{3,33},{4,4},{5,5},{6,36},{7,37},{8,8},{9,9},{1... | collective-permute-start | bytes 344072 | tf_op jit(solution)/shard_map/ppermute | solution.py:32
  137.7 2.1 %collective-permute-done.27 = f32[32,896]{1,0:T(8,128)S(1)} collective-permute-done((f32[32,896]{1,0:T(8,128)S(1)}, f32[32,896]{1,0:T(8,128)S(1)}, u32[]{:S(2)}, u32[]{:S(2)}) %collective-permute-start.27) | collective-permute-done | bytes 114720 | tf_op jit(solution)/shard_map/ppermute | solution.py:32
  139.7 1.1 collective-permute-done.26
  141.0 1.0 copy.3
  (56 shorter events, 1.6 us)
Async XLA Ops:
  0.0 3.2 %slice-start = ((bf16[32,8,16,128]{3,2,1,0:T(8,128)(2,1)}), bf16[32,4,16,128]{3,2,1,0:T(8,128)(2,1)S(1)}, s32[]{:S(2)}) async-start(bf16[32,8,16,128]{3,2,1,0:T(8,128)(2,1)} %param.3), calls=%async_computation | async-start | bytes 1048576 | tf_op jit(solution)/shard_map/slice | solution.py:241
  1.1 4.6 %copy-start.1 = (bf16[32,8,16,128]{3,2,1,0:T(8,128)(2,1)S(1)}, bf16[32,8,16,128]{3,2,1,0:T(8,128)(2,1)}, u32[]{:S(2)}) copy-start(bf16[32,8,16,128]{3,2,1,0:T(8,128)(2,1)} %param.2) | copy-start | bytes 3145732
  1.5 15.7 %collective-permute-start.2 = (bf16[32,8192]{1,0:T(8,128)(2,1)S(1)}, bf16[32,8192]{1,0:T(8,128)(2,1)S(1)}, u32[]{:S(2)}, u32[]{:S(2)}) collective-permute-start(bf16[32,8192]{1,0:T(8,128)(2,1)S(1)} %bitcast.40), channel_id=1, source_target_pairs={{0,4},{1,5},{2,6},{3,7},{4,0},{5,1},{6,2},{7,3},{8,12},{9,13},{10,... | collective-permute-start | bytes 1572872 | tf_op jit(solution)/shard_map/ppermute | solution.py:32
  3.5 16.1 %collective-permute-start.3 = (bf16[32,8192]{1,0:T(8,128)(2,1)S(1)}, bf16[32,8192]{1,0:T(8,128)(2,1)S(1)}, u32[]{:S(2)}, u32[]{:S(2)}) collective-permute-start(bf16[32,8192]{1,0:T(8,128)(2,1)S(1)} %bitcast.45), channel_id=1, source_target_pairs={{0,12},{1,13},{2,14},{3,15},{4,8},{5,9},{6,10},{7,11},{8,4},{9,5},... | collective-permute-start | bytes 1572872 | tf_op jit(solution)/shard_map/ppermute | solution.py:32
  6.5 6.3 %collective-permute-start.4 = (bf16[32,2048]{1,0:T(8,128)(2,1)S(1)}, bf16[32,2048]{1,0:T(8,128)(2,1)S(1)}, u32[]{:S(2)}, u32[]{:S(2)}) collective-permute-start(bf16[32,2048]{1,0:T(8,128)(2,1)S(1)} %get-tuple-element.64), channel_id=1, source_target_pairs={{0,16},{1,17},{2,18},{3,19},{4,20},{5,21},{6,22},{7,23},{8,24},{9,... | collective-permute-start | bytes 393224 | tf_op jit(solution)/shard_map/ppermute | solution.py:257
  10.3 6.9 %collective-permute-start.5 = (bf16[32,2048]{1,0:T(8,128)(2,1)S(1)}, bf16[32,2048]{1,0:T(8,128)(2,1)S(1)}, u32[]{:S(2)}, u32[]{:S(2)}) collective-permute-start(bf16[32,2048]{1,0:T(8,128)(2,1)S(1)} %get-tuple-element.63), channel_id=1, source_target_pairs={{16,0},{17,1},{18,2},{19,3},{20,4},{21,5},{22,6},{23,7},{24,8},{25... | collective-permute-start | bytes 393224 | tf_op jit(solution)/shard_map/ppermute | solution.py:257
  11.6 14.9 %collective-permute-start.6 = (bf16[32,8192]{1,0:T(8,128)(2,1)S(1)}, bf16[32,8192]{1,0:T(8,128)(2,1)S(1)}, u32[]{:S(2)}, u32[]{:S(2)}) collective-permute-start(bf16[32,8192]{1,0:T(8,128)(2,1)S(1)} %bitcast.46), channel_id=1, source_target_pairs={{0,4},{1,5},{2,6},{3,7},{4,0},{5,1},{6,2},{7,3},{8,12},{9,13},{10,... | collective-permute-start | bytes 1572872 | tf_op jit(solution)/shard_map/ppermute | solution.py:32
  12.8 16.6 %collective-permute-start.7 = (bf16[32,8192]{1,0:T(8,128)(2,1)S(1)}, bf16[32,8192]{1,0:T(8,128)(2,1)S(1)}, u32[]{:S(2)}, u32[]{:S(2)}) collective-permute-start(bf16[32,8192]{1,0:T(8,128)(2,1)S(1)} %bitcast.41), channel_id=1, source_target_pairs={{0,12},{1,13},{2,14},{3,15},{4,8},{5,9},{6,10},{7,11},{8,4},{9,5},... | collective-permute-start | bytes 1572872 | tf_op jit(solution)/shard_map/ppermute | solution.py:32
  17.2 12.8 %collective-permute-start = (bf16[32,8192]{1,0:T(8,128)(2,1)S(1)}, bf16[32,8192]{1,0:T(8,128)(2,1)S(1)}, u32[]{:S(2)}, u32[]{:S(2)}) collective-permute-start(bf16[32,8192]{1,0:T(8,128)(2,1)S(1)} %bitcast.42), channel_id=1, source_target_pairs={{0,1},{1,0},{2,3},{3,2},{4,5},{5,4},{6,7},{7,6},{8,9},{9,8},{10,11... | collective-permute-start | bytes 1572872 | tf_op jit(solution)/shard_map/ppermute | solution.py:32
  17.2 19.9 %copy-start.2 = (bf16[32,8192]{1,0:T(8,128)(2,1)}, bf16[32,8192]{1,0:T(8,128)(2,1)S(1)}, u32[]{:S(2)}) copy-start(bf16[32,8192]{1,0:T(8,128)(2,1)S(1)} %collective-permute-done.2.refs_4_) | copy-start | bytes 1572868
  17.2 13.3 %collective-permute-start.1 = (bf16[32,8192]{1,0:T(8,128)(2,1)S(1)}, bf16[32,8192]{1,0:T(8,128)(2,1)S(1)}, u32[]{:S(2)}, u32[]{:S(2)}) collective-permute-start(bf16[32,8192]{1,0:T(8,128)(2,1)S(1)} %bitcast.47), channel_id=1, source_target_pairs={{0,1},{1,0},{2,3},{3,2},{4,5},{5,4},{6,7},{7,6},{8,9},{9,8},{10,11... | collective-permute-start | bytes 1572872 | tf_op jit(solution)/shard_map/ppermute | solution.py:32
  19.6 19.8 %copy-start.3 = (bf16[32,8192]{1,0:T(8,128)(2,1)}, bf16[32,8192]{1,0:T(8,128)(2,1)S(1)}, u32[]{:S(2)}) copy-start(bf16[32,8192]{1,0:T(8,128)(2,1)S(1)} %collective-permute-done.3.refs_9_) | copy-start | bytes 1572868
  26.5 13.2 %copy-start.4 = (bf16[32,8192]{1,0:T(8,128)(2,1)}, bf16[32,8192]{1,0:T(8,128)(2,1)S(1)}, u32[]{:S(2)}) copy-start(bf16[32,8192]{1,0:T(8,128)(2,1)S(1)} %collective-permute-done.6.refs_5_) | copy-start | bytes 1572868
  29.4 10.2 %copy-start.5 = (bf16[32,8192]{1,0:T(8,128)(2,1)}, bf16[32,8192]{1,0:T(8,128)(2,1)S(1)}, u32[]{:S(2)}) copy-start(bf16[32,8192]{1,0:T(8,128)(2,1)S(1)} %collective-permute-done.7.refs_8_) | copy-start | bytes 1572868
  29.4 1.9 %collective-permute-start.8 = (bf16[32,8192]{1,0:T(8,128)(2,1)S(1)}, bf16[32,8192]{1,0:T(8,128)(2,1)S(1)}, u32[]{:S(2)}, u32[]{:S(2)}) collective-permute-start(bf16[32,8192]{1,0:T(8,128)(2,1)S(1)} %collective-permute-done.2.refs_4_), channel_id=1, source_target_pairs={{0,1},{1,0},{2,3},{3,2},{4,5},{5,4},{6,7},{7,6},{8,9},{9,8},{10,11... | collective-permute-start | bytes 1572872 | tf_op jit(solution)/shard_map/ppermute | solution.py:32
  29.4 6.3 %collective-permute-start.9 = (bf16[32,8192]{1,0:T(8,128)(2,1)S(1)}, bf16[32,8192]{1,0:T(8,128)(2,1)S(1)}, u32[]{:S(2)}, u32[]{:S(2)}) collective-permute-start(bf16[32,8192]{1,0:T(8,128)(2,1)S(1)} %collective-permute-done.6.refs_5_), channel_id=1, source_target_pairs={{0,1},{1,0},{2,3},{3,2},{4,5},{5,4},{6,7},{7,6},{8,9},{9,8},{10,11... | collective-permute-start | bytes 1572872 | tf_op jit(solution)/shard_map/ppermute | solution.py:32
  30.0 7.1 %collective-permute-start.10 = (bf16[32,8192]{1,0:T(8,128)(2,1)S(1)}, bf16[32,8192]{1,0:T(8,128)(2,1)S(1)}, u32[]{:S(2)}, u32[]{:S(2)}) collective-permute-start(bf16[32,8192]{1,0:T(8,128)(2,1)S(1)} %collective-permute-done.7.refs_8_), channel_id=1, source_target_pairs={{0,1},{1,0},{2,3},{3,2},{4,5},{5,4},{6,7},{7,6},{8,9},{9,8},{10,11... | collective-permute-start | bytes 1572872 | tf_op jit(solution)/shard_map/ppermute | solution.py:32
  30.0 9.4 %collective-permute-start.11 = (bf16[32,8192]{1,0:T(8,128)(2,1)S(1)}, bf16[32,8192]{1,0:T(8,128)(2,1)S(1)}, u32[]{:S(2)}, u32[]{:S(2)}) collective-permute-start(bf16[32,8192]{1,0:T(8,128)(2,1)S(1)} %collective-permute-done.3.refs_9_), channel_id=1, source_target_pairs={{0,1},{1,0},{2,3},{3,2},{4,5},{5,4},{6,7},{7,6},{8,9},{9,8},{10,11... | collective-permute-start | bytes 1572872 | tf_op jit(solution)/shard_map/ppermute | solution.py:32
  30.5 9.2 %copy-start.6 = (bf16[32,8192]{1,0:T(8,128)(2,1)}, bf16[32,8192]{1,0:T(8,128)(2,1)S(1)}, u32[]{:S(2)}) copy-start(bf16[32,8192]{1,0:T(8,128)(2,1)S(1)} %collective-permute-done.1.refs_3_) | copy-start | bytes 1572868
  30.5 28.0 %collective-permute-start.14 = (bf16[32,16384]{1,0:T(8,128)(2,1)S(1)}, bf16[32,16384]{1,0:T(8,128)(2,1)S(1)}, u32[]{:S(2)}, u32[]{:S(2)}) collective-permute-start(bf16[32,16384]{1,0:T(8,128)(2,1)S(1)} %bitcast.39), channel_id=1, source_target_pairs={{0,2},{1,3},{2,0},{3,1},{4,6},{5,7},{6,4},{7,5},{8,10},{9,11},{10,... | collective-permute-start | bytes 3145736 | tf_op jit(solution)/shard_map/ppermute | solution.py:32
  31.4 8.4 %copy-start.7 = (bf16[32,8192]{1,0:T(8,128)(2,1)}, bf16[32,8192]{1,0:T(8,128)(2,1)S(1)}, u32[]{:S(2)}) copy-start(bf16[32,8192]{1,0:T(8,128)(2,1)S(1)} %collective-permute-done.8.refs_6_) | copy-start | bytes 1572868
  31.4 21.0 %collective-permute-start.15 = (bf16[32,2048]{1,0:T(8,128)(2,1)S(1)}, bf16[32,2048]{1,0:T(8,128)(2,1)S(1)}, u32[]{:S(2)}, u32[]{:S(2)}) collective-permute-start(bf16[32,2048]{1,0:T(8,128)(2,1)S(1)} %get-tuple-element.64), channel_id=1, source_target_pairs={{0,18},{1,19},{2,16},{3,17},{4,22},{5,23},{6,20},{7,21},{8,26},{9,... | collective-permute-start | bytes 393224 | tf_op jit(solution)/shard_map/ppermute | solution.py:257
  35.8 3.9 %copy-start.8 = (bf16[32,8192]{1,0:T(8,128)(2,1)}, bf16[32,8192]{1,0:T(8,128)(2,1)S(1)}, u32[]{:S(2)}) copy-start(bf16[32,8192]{1,0:T(8,128)(2,1)S(1)} %collective-permute-done.9.refs_7_) | copy-start | bytes 1572868
  35.8 16.6 %collective-permute-start.16 = (bf16[32,2048]{1,0:T(8,128)(2,1)S(1)}, bf16[32,2048]{1,0:T(8,128)(2,1)S(1)}, u32[]{:S(2)}, u32[]{:S(2)}) collective-permute-start(bf16[32,2048]{1,0:T(8,128)(2,1)S(1)} %get-tuple-element.63), channel_id=1, source_target_pairs={{16,2},{17,3},{18,0},{19,1},{20,6},{21,7},{22,4},{23,5},{24,10},{2... | collective-permute-start | bytes 393224 | tf_op jit(solution)/shard_map/ppermute | solution.py:257
  37.1 2.6 %copy-start.9 = (bf16[32,8192]{1,0:T(8,128)(2,1)}, bf16[32,8192]{1,0:T(8,128)(2,1)S(1)}, u32[]{:S(2)}) copy-start(bf16[32,8192]{1,0:T(8,128)(2,1)S(1)} %collective-permute-done.10.refs_10_) | copy-start | bytes 1572868
  37.1 26.0 %collective-permute-start.12 = (bf16[32,8192]{1,0:T(8,128)(2,1)S(1)}, bf16[32,8192]{1,0:T(8,128)(2,1)}, u32[]{:S(2)}, u32[]{:S(2)}) collective-permute-start(bf16[32,8192]{1,0:T(8,128)(2,1)S(1)} %collective-permute-done.2.refs_4_), channel_id=1, source_target_pairs={{0,12},{1,13},{2,14},{3,15},{4,8},{5,9},{6,10},{7,11},{8,4},{9,5},... | collective-permute-start | bytes 1572872 | tf_op jit(solution)/shard_map/ppermute | solution.py:32
  39.4 0.8 copy-start.10
  39.4 23.7 %collective-permute-start.13 = (bf16[32,8192]{1,0:T(8,128)(2,1)S(1)}, bf16[32,8192]{1,0:T(8,128)(2,1)}, u32[]{:S(2)}, u32[]{:S(2)}) collective-permute-start(bf16[32,8192]{1,0:T(8,128)(2,1)S(1)} %collective-permute-done.3.refs_9_), channel_id=1, source_target_pairs={{0,4},{1,5},{2,6},{3,7},{4,0},{5,1},{6,2},{7,3},{8,12},{9,13},{10,... | collective-permute-start | bytes 1572872 | tf_op jit(solution)/shard_map/ppermute | solution.py:32
  63.1 2.1 %collective-permute-start.17 = (bf16[32,8192]{1,0:T(8,128)(2,1)}, bf16[32,8192]{1,0:T(8,128)(2,1)S(1)}, u32[]{:S(2)}, u32[]{:S(2)}) collective-permute-start(bf16[32,8192]{1,0:T(8,128)(2,1)} %collective-permute-done.12.refs_12_), channel_id=1, source_target_pairs={{0,1},{1,0},{2,3},{3,2},{4,5},{5,4},{6,7},{7,6},{8,9},{9,8},{10,11... | collective-permute-start | bytes 1572872 | tf_op jit(solution)/shard_map/ppermute | solution.py:32
  63.1 2.9 %collective-permute-start.18 = (bf16[32,8192]{1,0:T(8,128)(2,1)}, bf16[32,8192]{1,0:T(8,128)(2,1)S(1)}, u32[]{:S(2)}, u32[]{:S(2)}) collective-permute-start(bf16[32,8192]{1,0:T(8,128)(2,1)} %collective-permute-done.13.refs_13_), channel_id=1, source_target_pairs={{0,1},{1,0},{2,3},{3,2},{4,5},{5,4},{6,7},{7,6},{8,9},{9,8},{10,11... | collective-permute-start | bytes 1572872 | tf_op jit(solution)/shard_map/ppermute | solution.py:32
  65.2 0.8 copy-start.11
  66.0 0.8 copy-start.12
  88.9 27.0 %copy-start = (f32[8,2,32,896]{3,2,1,0:T(8,128)S(1)}, f32[8,2,32,896]{3,2,1,0:T(8,128)}, u32[]{:S(2)}) copy-start(f32[8,2,32,896]{3,2,1,0:T(8,128)} %shard_map.31) | copy-start | bytes 5505028
  90.1 11.1 %collective-permute-start.20 = (f32[2,32,896]{2,1,0:T(8,128)S(1)}, f32[2,32,896]{2,1,0:T(8,128)S(1)}, u32[]{:S(2)}, u32[]{:S(2)}) collective-permute-start(f32[2,32,896]{2,1,0:T(8,128)S(1)} %get-tuple-element.61), channel_id=1, source_target_pairs={{0,112},{1,113},{2,114},{3,115},{4,116},{5,117},{6,118},{7,119},{8... | collective-permute-start | bytes 688136 | tf_op jit(solution)/shard_map/ppermute | solution.py:32
  96.0 9.4 %collective-permute-start.19 = (f32[2,32,896]{2,1,0:T(8,128)S(1)}, f32[2,32,896]{2,1,0:T(8,128)S(1)}, u32[]{:S(2)}, u32[]{:S(2)}) collective-permute-start(f32[2,32,896]{2,1,0:T(8,128)S(1)} %get-tuple-element.62), channel_id=1, source_target_pairs={{0,16},{1,17},{2,18},{3,19},{4,20},{5,21},{6,22},{7,23},{8,24},{9,... | collective-permute-start | bytes 688136 | tf_op jit(solution)/shard_map/ppermute | solution.py:32
  106.6 6.9 %collective-permute-start.22 = (f32[2,32,896]{2,1,0:T(8,128)S(1)}, f32[2,32,896]{2,1,0:T(8,128)S(1)}, u32[]{:S(2)}, u32[]{:S(2)}) collective-permute-start(f32[2,32,896]{2,1,0:T(8,128)S(1)} %get-tuple-element.52), channel_id=1, source_target_pairs={{0,112},{1,113},{2,114},{3,115},{4,116},{5,117},{6,118},{7,119},{8... | collective-permute-start | bytes 688136 | tf_op jit(solution)/shard_map/ppermute | solution.py:32
  108.4 7.4 %collective-permute-start.21 = (f32[2,32,896]{2,1,0:T(8,128)S(1)}, f32[2,32,896]{2,1,0:T(8,128)S(1)}, u32[]{:S(2)}, u32[]{:S(2)}) collective-permute-start(f32[2,32,896]{2,1,0:T(8,128)S(1)} %get-tuple-element.51), channel_id=1, source_target_pairs={{0,16},{1,17},{2,18},{3,19},{4,20},{5,21},{6,22},{7,23},{8,24},{9,... | collective-permute-start | bytes 688136 | tf_op jit(solution)/shard_map/ppermute | solution.py:32
  115.9 7.3 %collective-permute-start.23 = (f32[2,32,896]{2,1,0:T(8,128)S(1)}, f32[2,32,896]{2,1,0:T(8,128)S(1)}, u32[]{:S(2)}, u32[]{:S(2)}) collective-permute-start(f32[2,32,896]{2,1,0:T(8,128)S(1)} %get-tuple-element.53), channel_id=1, source_target_pairs={{0,16},{1,17},{2,18},{3,19},{4,20},{5,21},{6,22},{7,23},{8,24},{9,... | collective-permute-start | bytes 688136 | tf_op jit(solution)/shard_map/ppermute | solution.py:32
  123.2 7.3 %collective-permute-start.24 = (f32[2,32,896]{2,1,0:T(8,128)S(1)}, f32[2,32,896]{2,1,0:T(8,128)S(1)}, u32[]{:S(2)}, u32[]{:S(2)}) collective-permute-start(f32[2,32,896]{2,1,0:T(8,128)S(1)} %bitcast_add_fusion.1), channel_id=1, source_target_pairs={{0,16},{1,17},{2,18},{3,19},{4,20},{5,21},{6,22},{7,23},{8,24},{9,... | collective-permute-start | bytes 688136 | tf_op jit(solution)/shard_map/ppermute | solution.py:32
  123.3 7.2 %collective-permute-start.25 = (f32[2,32,896]{2,1,0:T(8,128)S(1)}, f32[2,32,896]{2,1,0:T(8,128)S(1)}, u32[]{:S(2)}, u32[]{:S(2)}) collective-permute-start(f32[2,32,896]{2,1,0:T(8,128)S(1)} %get-tuple-element.56), channel_id=1, source_target_pairs={{0,112},{1,113},{2,114},{3,115},{4,116},{5,117},{6,118},{7,119},{8... | collective-permute-start | bytes 688136 | tf_op jit(solution)/shard_map/ppermute | solution.py:32
  130.6 9.1 %collective-permute-start.27 = (f32[32,896]{1,0:T(8,128)S(1)}, f32[32,896]{1,0:T(8,128)S(1)}, u32[]{:S(2)}, u32[]{:S(2)}) collective-permute-start(f32[32,896]{1,0:T(8,128)S(1)} %get-tuple-element.66), channel_id=1, source_target_pairs={{0,128},{1,129},{2,160},{3,161},{4,132},{5,133},{6,164},{7,165},{8... | collective-permute-start | bytes 344072 | tf_op jit(solution)/shard_map/ppermute | solution.py:32
  132.3 8.5 %collective-permute-start.26 = (f32[32,896]{1,0:T(8,128)S(1)}, f32[32,896]{1,0:T(8,128)S(1)}, u32[]{:S(2)}, u32[]{:S(2)}) collective-permute-start(f32[32,896]{1,0:T(8,128)S(1)} %get-tuple-element.65), channel_id=1, source_target_pairs={{0,0},{1,1},{2,32},{3,33},{4,4},{5,5},{6,36},{7,37},{8,8},{9,9},{1... | collective-permute-start | bytes 344072 | tf_op jit(solution)/shard_map/ppermute | solution.py:32

commit v2 on v0

--- a/solution.py
+++ b/solution.py
@@ -89,19 +89,32 @@
     rows = held.shape[0] // count
     tall = count * rows
 
+    def arrivals(at):
+        copies = []
+        for i, parts in enumerate(blocks):
+            part, inner = divmod(at, slabs // len(parts))
+            copies.append(
+                pltpu.make_async_copy(
+                    parts[part].at[:, pl.ds(inner * lanes, lanes)],
+                    held.at[pl.ds(i * rows, rows), pl.ds(at * lanes, lanes)],
+                    sems.at[i, at],
+                )
+            )
+        return copies
+
     @pl.when(x == 0)
     def _():
-        copies = []
-        for i, parts in enumerate(blocks):
-            width = held.shape[1] // len(parts)
-            for j, part in enumerate(parts):
-                to = held.at[pl.ds(i * rows, rows), pl.ds(j * width, width)]
-                copies.append(pltpu.make_async_copy(part, to, sems.at[len(copies)]))
-        for copy in copies:
-            copy.start()
+        for at in range(slabs):
+            for copy in arrivals(at):
+                copy.start()
         total[...] = jnp.zeros_like(total)
-        for copy in copies:
+
+    def arrived(at):
+        for copy in arrivals(at):
             copy.wait()
+
+    for at in range(slabs):
+        pl.when(x == at)(functools.partial(arrived, at))
 
     def add(first, last):
         left = jnp.concatenate(
@@ -158,7 +171,7 @@
         scratch_shapes=[
             pltpu.VMEM((count * rows, cells), own.dtype),
             pltpu.VMEM((3, 3 * count * rows, 2 * own.shape[2]), jnp.float32),
-            pltpu.SemaphoreType.DMA((sum(cuts),)),
+            pltpu.SemaphoreType.DMA((count, slabs)),
         ],
         compiler_params=pltpu.CompilerParams(vmem_limit_bytes=VMEM),
         cost_estimate=pl.CostEstimate(
@@ -173,7 +186,6 @@
         up = shift(up, z=1) + piece(step)
         if step > 1:
             down = shift(down, z=-1) + piece(1 - step)
-        up, down = lax.optimization_barrier((up, down))
     return shift(up, z=1) + shift(down, z=-1) + piece(0)
 
 
@@ -221,11 +233,9 @@
         (next_one, last_two, next_two, last_one, own)
     )
     mates = [shift(v, k=1) for v in (one, two, next_one, last_two, next_two, last_one)]
-    far_one, far_two, acts_near, near_ends, own, mates = lax.optimization_barrier(
-        (far_one, far_two, acts_near, near_ends, own, mates)
-    )
+    near = spread(acts_near, jnp.concatenate(near_ends, axis=1), size_z, lanes)
+    far_one, far_two, near, mates = lax.optimization_barrier((far_one, far_two, near, mates))
     far_mate = shift(far_one, k=1), shift(far_two, k=1)
-    near = spread(acts_near, jnp.concatenate(near_ends, axis=1), size_z, lanes)
     blocks = (
         (one, two),
         (mates[0], mates[1]),

time: 146 us -> 140 us (0.959)
  waiting for transfers between devices: 61.8 us -> 50.1 us
  starting transfers between devices: 37.2 us -> 44.2 us
    ppermute x4, waiting for transfers between devices: 14.3 us -> 2.08 us  [move(): return lax.ppermute(value, AXES, pairs)]
    ppermute x24, starting transfers between devices: 27 us -> 33.3 us  [send(): return lax.ppermute(value, AXES, pairs)]
    unnamed x27 -> x29, local copies, waits for them, and re-layouts: 3.32 us -> 3.55 us
  transfers between devices with their start and end apart: 28 -> 28, of which waited for: 14 -> 14; matrix products, arithmetic and copies ran while one was open for 1% -> 1% of each run, Pallas kernels for 6% -> 7%
where the time goes in v2:
time: 140 us; the launch traced here: 139 us
  waiting for transfers between devices  50.1 us (36%)
  starting transfers between devices  44.2 us (32%)
  Pallas kernels  35.8 us (26%)
  local copies, waits for them, and re-layouts  7.16 us (5%)
    ppermute x24, waiting for transfers between devices, send(): return lax.ppermute(value, AXES, pairs)  48 us
    ppermute x24, starting transfers between devices, send(): return lax.ppermute(value, AXES, pairs)  33.3 us
    pallas_call x1, Pallas kernels, product(): pl.pallas_call(functools.partial(product_body, cuts, slabs, size_z), grid...  26.5 us
    ppermute x4, starting transfers between devices, move(): return lax.ppermute(value, AXES, pairs)  10.9 us
    pallas_call x2, Pallas kernels, spread(): pl.pallas_call(functools.partial(spread_body, size_z, slabs, lanes), grid...  9.32 us
    unnamed x29, local copies, waits for them, and re-layouts  3.55 us
  transfers between devices with their start and end apart: 28, of which 14 were waited for; matrix products, arithmetic and copies ran while one was open for 1% of the time, Pallas kernels for 7%

profile of v2, /device:TPU:2, one launch (start us, length us, event | category | flops | bytes accessed | tf_op | source)
XLA Modules:
  0.0 138.9 jit_solution(9749580016721897835)
XLA Ops:
  0.0 1.1 slice.17
  1.2 0.3 copy.12
  1.5 1.7 %collective-permute-start = (bf16[32,8192]{1,0:T(8,128)(2,1)S(1)}, bf16[32,8192]{1,0:T(8,128)(2,1)S(1)}, u32[]{:S(2)}, u32[]{:S(2)}) collective-permute-start(bf16[32,8192]{1,0:T(8,128)(2,1)S(1)} %bitcast.40), channel_id=1, source_target_pairs={{0,4},{1,5},{2,6},{3,7},{4,0},{5,1},{6,2},{7,3},{8,12},{9,13},{10,... | collective-permute-start | bytes 1572872 | tf_op jit(solution)/shard_map/ppermute | solution.py:32
  3.2 0.3 copy.11
  3.5 0.7 copy.10
  4.2 3.8 %collective-permute-start.2 = (bf16[32,2048]{1,0:T(8,128)(2,1)S(1)}, bf16[32,2048]{1,0:T(8,128)(2,1)S(1)}, u32[]{:S(2)}, u32[]{:S(2)}) collective-permute-start(bf16[32,2048]{1,0:T(8,128)(2,1)S(1)} %get-tuple-element.56), channel_id=1, source_target_pairs={{0,16},{1,17},{2,18},{3,19},{4,20},{5,21},{6,22},{7,23},{8,24},{9,... | collective-permute-start | bytes 393224 | tf_op jit(solution)/shard_map/ppermute | solution.py:224
  8.1 1.3 collective-permute-start.3
  9.4 2.3 %collective-permute-start.1 = (bf16[32,8192]{1,0:T(8,128)(2,1)S(1)}, bf16[32,8192]{1,0:T(8,128)(2,1)S(1)}, u32[]{:S(2)}, u32[]{:S(2)}) collective-permute-start(bf16[32,8192]{1,0:T(8,128)(2,1)S(1)} %bitcast.44), channel_id=1, source_target_pairs={{0,12},{1,13},{2,14},{3,15},{4,8},{5,9},{6,10},{7,11},{8,4},{9,5},... | collective-permute-start | bytes 1572872 | tf_op jit(solution)/shard_map/ppermute | solution.py:32
  11.7 0.7 collective-permute-start.11
  12.3 0.5 collective-permute-start.6
  12.9 2.1 %collective-permute-done.3 = bf16[32,2048]{1,0:T(8,128)(2,1)S(1)} collective-permute-done((bf16[32,2048]{1,0:T(8,128)(2,1)S(1)}, bf16[32,2048]{1,0:T(8,128)(2,1)S(1)}, u32[]{:S(2)}, u32[]{:S(2)}) %collective-permute-start.3) | collective-permute-done | bytes 131104 | tf_op jit(solution)/shard_map/ppermute | solution.py:224
  14.9 2.2 %collective-permute-start.12 = (bf16[32,8192]{1,0:T(8,128)(2,1)S(1)}, bf16[32,8192]{1,0:T(8,128)(2,1)S(1)}, u32[]{:S(2)}, u32[]{:S(2)}) collective-permute-start(bf16[32,8192]{1,0:T(8,128)(2,1)S(1)} %bitcast.41), channel_id=1, source_target_pairs={{0,12},{1,13},{2,14},{3,15},{4,8},{5,9},{6,10},{7,11},{8,4},{9,5},... | collective-permute-start | bytes 1572872 | tf_op jit(solution)/shard_map/ppermute | solution.py:32
  17.1 1.3 collective-permute-start.8
  18.4 7.1 %collective-permute-done.1.refs_13_ = bf16[32,8192]{1,0:T(8,128)(2,1)S(1)} collective-permute-done((bf16[32,8192]{1,0:T(8,128)(2,1)S(1)}, bf16[32,8192]{1,0:T(8,128)(2,1)S(1)}, u32[]{:S(2)}, u32[]{:S(2)}) %collective-permute-start.1) | collective-permute-done | bytes 524320 | tf_op jit(solution)/shard_map/ppermute | solution.py:32
  25.5 0.5 collective-permute-start.10
  26.0 0.5 collective-permute-done.11.refs_5_
  26.5 3.0 %collective-permute-start.4 = (bf16[32,8192]{1,0:T(8,128)(2,1)S(1)}, bf16[32,8192]{1,0:T(8,128)(2,1)}, u32[]{:S(2)}, u32[]{:S(2)}) collective-permute-start(bf16[32,8192]{1,0:T(8,128)(2,1)S(1)} %collective-permute-done.refs_4_), channel_id=1, source_target_pairs={{0,12},{1,13},{2,14},{3,15},{4,8},{5,9},{6,10},{7,11},{8,4},{9,5},... | collective-permute-start | bytes 1572872 | tf_op jit(solution)/shard_map/ppermute | solution.py:32
  29.5 7.2 %collective-permute-done.12.refs_12_ = bf16[32,8192]{1,0:T(8,128)(2,1)S(1)} collective-permute-done((bf16[32,8192]{1,0:T(8,128)(2,1)S(1)}, bf16[32,8192]{1,0:T(8,128)(2,1)S(1)}, u32[]{:S(2)}, u32[]{:S(2)}) %collective-permute-start.12) | collective-permute-done | bytes 524320 | tf_op jit(solution)/shard_map/ppermute | solution.py:32
  36.7 4.5 %collective-permute-start.7 = (bf16[32,2048]{1,0:T(8,128)(2,1)S(1)}, bf16[32,2048]{1,0:T(8,128)(2,1)S(1)}, u32[]{:S(2)}, u32[]{:S(2)}) collective-permute-start(bf16[32,2048]{1,0:T(8,128)(2,1)S(1)} %get-tuple-element.56), channel_id=1, source_target_pairs={{0,18},{1,19},{2,16},{3,17},{4,22},{5,23},{6,20},{7,21},{8,26},{9,... | collective-permute-start | bytes 393224 | tf_op jit(solution)/shard_map/ppermute | solution.py:224
  41.3 4.7 %shard_map.29.refs_16_ = bf16[10,2304,128]{2,1,0:T(8,128)(2,1)} custom-call(bf16[32,16384]{1,0:T(8,128)(2,1)S(1)} %bitcast.39, bf16[32,4096]{1,0:T(8,128)(2,1)S(1)} %pad_maximum_fusion.1.edge), custom_call_target="tpu_custom_call" | custom-call | flops 10485760 | bytes 10485760 | tf_op jit(solution)/shard_map/pallas_call | solution.py:66
  46.1 0.6 collective-permute-start.14
  46.8 0.4 collective-permute-start.16
  47.2 4.6 %shard_map.28.refs_17_ = bf16[10,2304,128]{2,1,0:T(8,128)(2,1)} custom-call(bf16[32,16384]{1,0:T(8,128)(2,1)S(1)} %collective-permute-done.6.middle, bf16[32,4096]{1,0:T(8,128)(2,1)S(1)} %pad_maximum_fusion.edge), custom_call_target="tpu_custom_call" | custom-call | flops 10485760 | bytes 10485760 | tf_op jit(solution)/shard_map/pallas_call | solution.py:66
  51.8 4.3 %collective-permute-done.5.refs_9_ = bf16[32,8192]{1,0:T(8,128)(2,1)} collective-permute-done((bf16[32,8192]{1,0:T(8,128)(2,1)S(1)}, bf16[32,8192]{1,0:T(8,128)(2,1)}, u32[]{:S(2)}, u32[]{:S(2)}) %collective-permute-start.5) | collective-permute-done | bytes 524320 | tf_op jit(solution)/shard_map/ppermute | solution.py:32
  56.2 0.8 copy-done.7
  57.2 0.3 collective-permute-start.18
  57.8 1.3 collective-permute-done.17.refs_10_
  59.1 0.7 collective-permute-done.18.refs_11_
  59.9 0.8 copy-done.12
  60.7 26.5 %shard_map.30 = f32[8,2,32,896]{3,2,1,0:T(8,128)} custom-call(bf16[32,8192]{1,0:T(8,128)(2,1)S(1)} %bitcast.43, bf16[32,8192]{1,0:T(8,128)(2,1)S(1)} %bitcast.47, bf16[32,8192]{1,0:T(8,128)(2,1)S(1)} %collective-permute-done.9.refs_2_, bf16[32,8192]{1,0:T(8,128)(2,1)} %copy-done.6, bf16[32,8192]{1,0:T(8,128)(2,1)} %copy-done.2, bf16[32,8192]{1,0:T(8,128)(2,1)} %copy-done.4, ...), custom_call_target="tpu_custom_call" | custom-call | flops 24000000000 | bytes 16777216 | tf_op jit(solution)/shard_map/pallas_call | solution.py:165
  87.3 1.2 dynamic-slice_bitcast_fusion
  88.5 2.0 %collective-permute-start.19 = (f32[2,32,896]{2,1,0:T(8,128)S(1)}, f32[2,32,896]{2,1,0:T(8,128)S(1)}, u32[]{:S(2)}, u32[]{:S(2)}) collective-permute-start(f32[2,32,896]{2,1,0:T(8,128)S(1)} %get-tuple-element.54), channel_id=1, source_target_pairs={{0,16},{1,17},{2,18},{3,19},{4,20},{5,21},{6,22},{7,23},{8,24},{9,... | collective-permute-start | bytes 688136 | tf_op jit(solution)/shard_map/ppermute | solution.py:32
  90.5 4.5 %collective-permute-start.23 = (f32[2,32,896]{2,1,0:T(8,128)S(1)}, f32[2,32,896]{2,1,0:T(8,128)S(1)}, u32[]{:S(2)}, u32[]{:S(2)}) collective-permute-start(f32[2,32,896]{2,1,0:T(8,128)S(1)} %get-tuple-element.53), channel_id=1, source_target_pairs={{0,112},{1,113},{2,114},{3,115},{4,116},{5,117},{6,118},{7,119},{8... | collective-permute-start | bytes 688136 | tf_op jit(solution)/shard_map/ppermute | solution.py:32
  95.0 5.7 %collective-permute-done.19 = f32[2,32,896]{2,1,0:T(8,128)S(1)} collective-permute-done((f32[2,32,896]{2,1,0:T(8,128)S(1)}, f32[2,32,896]{2,1,0:T(8,128)S(1)}, u32[]{:S(2)}, u32[]{:S(2)}) %collective-permute-start.19) | collective-permute-done | bytes 229408 | tf_op jit(solution)/shard_map/ppermute | solution.py:32
  100.7 1.0 bitcast_add_fusion.5
  101.9 8.1 %collective-permute-done.20 = f32[2,32,896]{2,1,0:T(8,128)S(1)} collective-permute-done((f32[2,32,896]{2,1,0:T(8,128)S(1)}, f32[2,32,896]{2,1,0:T(8,128)S(1)}, u32[]{:S(2)}, u32[]{:S(2)}) %collective-permute-start.20) | collective-permute-done | bytes 229408 | tf_op jit(solution)/shard_map/ppermute | solution.py:32
  110.1 0.3 collective-permute-start.24
  110.4 1.8 %collective-permute-start.21 = (f32[2,32,896]{2,1,0:T(8,128)S(1)}, f32[2,32,896]{2,1,0:T(8,128)S(1)}, u32[]{:S(2)}, u32[]{:S(2)}) collective-permute-start(f32[2,32,896]{2,1,0:T(8,128)S(1)} %get-tuple-element.52), channel_id=1, source_target_pairs={{0,16},{1,17},{2,18},{3,19},{4,20},{5,21},{6,22},{7,23},{8,24},{9,... | collective-permute-start | bytes 688136 | tf_op jit(solution)/shard_map/ppermute | solution.py:32
  112.2 4.2 %collective-permute-done.24 = f32[2,32,896]{2,1,0:T(8,128)S(1)} collective-permute-done((f32[2,32,896]{2,1,0:T(8,128)S(1)}, f32[2,32,896]{2,1,0:T(8,128)S(1)}, u32[]{:S(2)}, u32[]{:S(2)}) %collective-permute-start.24) | collective-permute-done | bytes 229408 | tf_op jit(solution)/shard_map/ppermute | solution.py:32
  116.4 1.3 collective-permute-done.21
  117.7 0.6 collective-permute-start.22
  118.3 2.7 %collective-permute-start.25 = (f32[2,32,896]{2,1,0:T(8,128)S(1)}, f32[2,32,896]{2,1,0:T(8,128)S(1)}, u32[]{:S(2)}, u32[]{:S(2)}) collective-permute-start(f32[2,32,896]{2,1,0:T(8,128)S(1)} %get-tuple-element.49), channel_id=1, source_target_pairs={{0,112},{1,113},{2,114},{3,115},{4,116},{5,117},{6,118},{7,119},{8... | collective-permute-start | bytes 688136 | tf_op jit(solution)/shard_map/ppermute | solution.py:32
  121.0 4.0 %collective-permute-done.22 = f32[2,32,896]{2,1,0:T(8,128)S(1)} collective-permute-done((f32[2,32,896]{2,1,0:T(8,128)S(1)}, f32[2,32,896]{2,1,0:T(8,128)S(1)}, u32[]{:S(2)}, u32[]{:S(2)}) %collective-permute-start.22) | collective-permute-done | bytes 229408 | tf_op jit(solution)/shard_map/ppermute | solution.py:32
  125.1 3.1 %collective-permute-start.27 = (f32[32,896]{1,0:T(8,128)S(1)}, f32[32,896]{1,0:T(8,128)S(1)}, u32[]{:S(2)}, u32[]{:S(2)}) collective-permute-start(f32[32,896]{1,0:T(8,128)S(1)} %get-tuple-element.58), channel_id=1, source_target_pairs={{0,128},{1,129},{2,160},{3,161},{4,132},{5,133},{6,164},{7,165},{8... | collective-permute-start | bytes 344072 | tf_op jit(solution)/shard_map/ppermute | solution.py:32
  128.2 5.9 %collective-permute-start.26 = (f32[32,896]{1,0:T(8,128)S(1)}, f32[32,896]{1,0:T(8,128)S(1)}, u32[]{:S(2)}, u32[]{:S(2)}) collective-permute-start(f32[32,896]{1,0:T(8,128)S(1)} %get-tuple-element.57), channel_id=1, source_target_pairs={{0,0},{1,1},{2,32},{3,33},{4,4},{5,5},{6,36},{7,37},{8,8},{9,9},{1... | collective-permute-start | bytes 344072 | tf_op jit(solution)/shard_map/ppermute | solution.py:32
  134.1 1.0 collective-permute-done.27
  135.1 2.5 %collective-permute-done.26 = f32[32,896]{1,0:T(8,128)S(1)} collective-permute-done((f32[32,896]{1,0:T(8,128)S(1)}, f32[32,896]{1,0:T(8,128)S(1)}, u32[]{:S(2)}, u32[]{:S(2)}) %collective-permute-start.26) | collective-permute-done | bytes 114720 | tf_op jit(solution)/shard_map/ppermute | solution.py:32
  137.8 1.0 copy.3
  (55 shorter events, 1.4 us)
Async XLA Ops:
  0.0 3.2 %slice-start = ((bf16[32,8,16,128]{3,2,1,0:T(8,128)(2,1)}), bf16[32,4,16,128]{3,2,1,0:T(8,128)(2,1)S(1)}, s32[]{:S(2)}) async-start(bf16[32,8,16,128]{3,2,1,0:T(8,128)(2,1)} %param.3), calls=%async_computation | async-start | bytes 1048576 | tf_op jit(solution)/shard_map/slice | solution.py:208
  1.1 2.4 %copy-start.1 = (bf16[32,8,16,128]{3,2,1,0:T(8,128)(2,1)S(1)}, bf16[32,8,16,128]{3,2,1,0:T(8,128)(2,1)}, u32[]{:S(2)}) copy-start(bf16[32,8,16,128]{3,2,1,0:T(8,128)(2,1)} %param.2) | copy-start | bytes 3145732
  1.5 15.6 %collective-permute-start = (bf16[32,8192]{1,0:T(8,128)(2,1)S(1)}, bf16[32,8192]{1,0:T(8,128)(2,1)S(1)}, u32[]{:S(2)}, u32[]{:S(2)}) collective-permute-start(bf16[32,8192]{1,0:T(8,128)(2,1)S(1)} %bitcast.40), channel_id=1, source_target_pairs={{0,4},{1,5},{2,6},{3,7},{4,0},{5,1},{6,2},{7,3},{8,12},{9,13},{10,... | collective-permute-start | bytes 1572872 | tf_op jit(solution)/shard_map/ppermute | solution.py:32
  4.2 8.1 %collective-permute-start.2 = (bf16[32,2048]{1,0:T(8,128)(2,1)S(1)}, bf16[32,2048]{1,0:T(8,128)(2,1)S(1)}, u32[]{:S(2)}, u32[]{:S(2)}) collective-permute-start(bf16[32,2048]{1,0:T(8,128)(2,1)S(1)} %get-tuple-element.56), channel_id=1, source_target_pairs={{0,16},{1,17},{2,18},{3,19},{4,20},{5,21},{6,22},{7,23},{8,24},{9,... | collective-permute-start | bytes 393224 | tf_op jit(solution)/shard_map/ppermute | solution.py:224
  8.1 6.9 %collective-permute-start.3 = (bf16[32,2048]{1,0:T(8,128)(2,1)S(1)}, bf16[32,2048]{1,0:T(8,128)(2,1)S(1)}, u32[]{:S(2)}, u32[]{:S(2)}) collective-permute-start(bf16[32,2048]{1,0:T(8,128)(2,1)S(1)} %get-tuple-element.55), channel_id=1, source_target_pairs={{16,0},{17,1},{18,2},{19,3},{20,4},{21,5},{22,6},{23,7},{24,8},{25... | collective-permute-start | bytes 393224 | tf_op jit(solution)/shard_map/ppermute | solution.py:224
  9.4 16.1 %collective-permute-start.1 = (bf16[32,8192]{1,0:T(8,128)(2,1)S(1)}, bf16[32,8192]{1,0:T(8,128)(2,1)S(1)}, u32[]{:S(2)}, u32[]{:S(2)}) collective-permute-start(bf16[32,8192]{1,0:T(8,128)(2,1)S(1)} %bitcast.44), channel_id=1, source_target_pairs={{0,12},{1,13},{2,14},{3,15},{4,8},{5,9},{6,10},{7,11},{8,4},{9,5},... | collective-permute-start | bytes 1572872 | tf_op jit(solution)/shard_map/ppermute | solution.py:32
  11.7 14.8 %collective-permute-start.11 = (bf16[32,8192]{1,0:T(8,128)(2,1)S(1)}, bf16[32,8192]{1,0:T(8,128)(2,1)S(1)}, u32[]{:S(2)}, u32[]{:S(2)}) collective-permute-start(bf16[32,8192]{1,0:T(8,128)(2,1)S(1)} %bitcast.45), channel_id=1, source_target_pairs={{0,4},{1,5},{2,6},{3,7},{4,0},{5,1},{6,2},{7,3},{8,12},{9,13},{10,... | collective-permute-start | bytes 1572872 | tf_op jit(solution)/shard_map/ppermute | solution.py:32
  12.3 34.5 %collective-permute-start.6 = (bf16[32,16384]{1,0:T(8,128)(2,1)S(1)}, bf16[32,16384]{1,0:T(8,128)(2,1)S(1)}, u32[]{:S(2)}, u32[]{:S(2)}) collective-permute-start(bf16[32,16384]{1,0:T(8,128)(2,1)S(1)} %bitcast.38), channel_id=1, source_target_pairs={{0,2},{1,3},{2,0},{3,1},{4,6},{5,7},{6,4},{7,5},{8,10},{9,11},{10,... | collective-permute-start | bytes 3145736 | tf_op jit(solution)/shard_map/ppermute | solution.py:32
  14.9 21.8 %collective-permute-start.12 = (bf16[32,8192]{1,0:T(8,128)(2,1)S(1)}, bf16[32,8192]{1,0:T(8,128)(2,1)S(1)}, u32[]{:S(2)}, u32[]{:S(2)}) collective-permute-start(bf16[32,8192]{1,0:T(8,128)(2,1)S(1)} %bitcast.41), channel_id=1, source_target_pairs={{0,12},{1,13},{2,14},{3,15},{4,8},{5,9},{6,10},{7,11},{8,4},{9,5},... | collective-permute-start | bytes 1572872 | tf_op jit(solution)/shard_map/ppermute | solution.py:32
  17.1 28.8 %copy-start.2 = (bf16[32,8192]{1,0:T(8,128)(2,1)}, bf16[32,8192]{1,0:T(8,128)(2,1)S(1)}, u32[]{:S(2)}) copy-start(bf16[32,8192]{1,0:T(8,128)(2,1)S(1)} %collective-permute-done.refs_4_) | copy-start | bytes 1572868
  17.1 8.4 %collective-permute-start.8 = (bf16[32,2048]{1,0:T(8,128)(2,1)S(1)}, bf16[32,2048]{1,0:T(8,128)(2,1)S(1)}, u32[]{:S(2)}, u32[]{:S(2)}) collective-permute-start(bf16[32,2048]{1,0:T(8,128)(2,1)S(1)} %get-tuple-element.55), channel_id=1, source_target_pairs={{16,2},{17,3},{18,0},{19,1},{20,6},{21,7},{22,4},{23,5},{24,10},{2... | collective-permute-start | bytes 393224 | tf_op jit(solution)/shard_map/ppermute | solution.py:224
  25.5 20.6 %copy-start.3 = (bf16[32,8192]{1,0:T(8,128)(2,1)}, bf16[32,8192]{1,0:T(8,128)(2,1)S(1)}, u32[]{:S(2)}) copy-start(bf16[32,8192]{1,0:T(8,128)(2,1)S(1)} %collective-permute-done.1.refs_13_) | copy-start | bytes 1572868
  25.5 20.5 %collective-permute-start.9 = (bf16[32,8192]{1,0:T(8,128)(2,1)S(1)}, bf16[32,8192]{1,0:T(8,128)(2,1)S(1)}, u32[]{:S(2)}, u32[]{:S(2)}) collective-permute-start(bf16[32,8192]{1,0:T(8,128)(2,1)S(1)} %bitcast.42), channel_id=1, source_target_pairs={{0,1},{1,0},{2,3},{3,2},{4,5},{5,4},{6,7},{7,6},{8,9},{9,8},{10,11... | collective-permute-start | bytes 1572872 | tf_op jit(solution)/shard_map/ppermute | solution.py:32
  25.5 20.6 %collective-permute-start.10 = (bf16[32,8192]{1,0:T(8,128)(2,1)S(1)}, bf16[32,8192]{1,0:T(8,128)(2,1)S(1)}, u32[]{:S(2)}, u32[]{:S(2)}) collective-permute-start(bf16[32,8192]{1,0:T(8,128)(2,1)S(1)} %bitcast.46), channel_id=1, source_target_pairs={{0,1},{1,0},{2,3},{3,2},{4,5},{5,4},{6,7},{7,6},{8,9},{9,8},{10,11... | collective-permute-start | bytes 1572872 | tf_op jit(solution)/shard_map/ppermute | solution.py:32
  26.5 20.2 %copy-start.4 = (bf16[32,8192]{1,0:T(8,128)(2,1)}, bf16[32,8192]{1,0:T(8,128)(2,1)S(1)}, u32[]{:S(2)}) copy-start(bf16[32,8192]{1,0:T(8,128)(2,1)S(1)} %collective-permute-done.11.refs_5_) | copy-start | bytes 1572868
  26.5 20.2 %collective-permute-start.4 = (bf16[32,8192]{1,0:T(8,128)(2,1)S(1)}, bf16[32,8192]{1,0:T(8,128)(2,1)}, u32[]{:S(2)}, u32[]{:S(2)}) collective-permute-start(bf16[32,8192]{1,0:T(8,128)(2,1)S(1)} %collective-permute-done.refs_4_), channel_id=1, source_target_pairs={{0,12},{1,13},{2,14},{3,15},{4,8},{5,9},{6,10},{7,11},{8,4},{9,5},... | collective-permute-start | bytes 1572872 | tf_op jit(solution)/shard_map/ppermute | solution.py:32
  36.7 10.1 %copy-start.5 = (bf16[32,8192]{1,0:T(8,128)(2,1)}, bf16[32,8192]{1,0:T(8,128)(2,1)S(1)}, u32[]{:S(2)}) copy-start(bf16[32,8192]{1,0:T(8,128)(2,1)S(1)} %collective-permute-done.12.refs_12_) | copy-start | bytes 1572868
  36.7 9.2 %collective-permute-start.7 = (bf16[32,2048]{1,0:T(8,128)(2,1)S(1)}, bf16[32,2048]{1,0:T(8,128)(2,1)S(1)}, u32[]{:S(2)}, u32[]{:S(2)}) collective-permute-start(bf16[32,2048]{1,0:T(8,128)(2,1)S(1)} %get-tuple-element.56), channel_id=1, source_target_pairs={{0,18},{1,19},{2,16},{3,17},{4,22},{5,23},{6,20},{7,21},{8,26},{9,... | collective-permute-start | bytes 393224 | tf_op jit(solution)/shard_map/ppermute | solution.py:224
  46.0 10.2 %collective-permute-start.5 = (bf16[32,8192]{1,0:T(8,128)(2,1)S(1)}, bf16[32,8192]{1,0:T(8,128)(2,1)}, u32[]{:S(2)}, u32[]{:S(2)}) collective-permute-start(bf16[32,8192]{1,0:T(8,128)(2,1)S(1)} %collective-permute-done.1.refs_13_), channel_id=1, source_target_pairs={{0,4},{1,5},{2,6},{3,7},{4,0},{5,1},{6,2},{7,3},{8,12},{9,13},{10,... | collective-permute-start | bytes 1572872 | tf_op jit(solution)/shard_map/ppermute | solution.py:32
  46.0 10.2 %collective-permute-start.13 = (bf16[32,8192]{1,0:T(8,128)(2,1)S(1)}, bf16[32,8192]{1,0:T(8,128)(2,1)S(1)}, u32[]{:S(2)}, u32[]{:S(2)}) collective-permute-start(bf16[32,8192]{1,0:T(8,128)(2,1)S(1)} %collective-permute-done.refs_4_), channel_id=1, source_target_pairs={{0,1},{1,0},{2,3},{3,2},{4,5},{5,4},{6,7},{7,6},{8,9},{9,8},{10,11... | collective-permute-start | bytes 1572872 | tf_op jit(solution)/shard_map/ppermute | solution.py:32
  46.1 5.7 %copy-start.6 = (bf16[32,8192]{1,0:T(8,128)(2,1)}, bf16[32,8192]{1,0:T(8,128)(2,1)S(1)}, u32[]{:S(2)}) copy-start(bf16[32,8192]{1,0:T(8,128)(2,1)S(1)} %collective-permute-done.10.refs_3_) | copy-start | bytes 1572868
  46.1 10.0 %collective-permute-start.14 = (bf16[32,8192]{1,0:T(8,128)(2,1)S(1)}, bf16[32,8192]{1,0:T(8,128)(2,1)S(1)}, u32[]{:S(2)}, u32[]{:S(2)}) collective-permute-start(bf16[32,8192]{1,0:T(8,128)(2,1)S(1)} %collective-permute-done.1.refs_13_), channel_id=1, source_target_pairs={{0,1},{1,0},{2,3},{3,2},{4,5},{5,4},{6,7},{7,6},{8,9},{9,8},{10,11... | collective-permute-start | bytes 1572872 | tf_op jit(solution)/shard_map/ppermute | solution.py:32
  46.7 9.5 %collective-permute-start.15 = (bf16[32,8192]{1,0:T(8,128)(2,1)S(1)}, bf16[32,8192]{1,0:T(8,128)(2,1)S(1)}, u32[]{:S(2)}, u32[]{:S(2)}) collective-permute-start(bf16[32,8192]{1,0:T(8,128)(2,1)S(1)} %collective-permute-done.11.refs_5_), channel_id=1, source_target_pairs={{0,1},{1,0},{2,3},{3,2},{4,5},{5,4},{6,7},{7,6},{8,9},{9,8},{10,11... | collective-permute-start | bytes 1572872 | tf_op jit(solution)/shard_map/ppermute | solution.py:32
  46.8 9.4 %collective-permute-start.16 = (bf16[32,8192]{1,0:T(8,128)(2,1)S(1)}, bf16[32,8192]{1,0:T(8,128)(2,1)S(1)}, u32[]{:S(2)}, u32[]{:S(2)}) collective-permute-start(bf16[32,8192]{1,0:T(8,128)(2,1)S(1)} %collective-permute-done.12.refs_12_), channel_id=1, source_target_pairs={{0,1},{1,0},{2,3},{3,2},{4,5},{5,4},{6,7},{7,6},{8,9},{9,8},{10,11... | collective-permute-start | bytes 1572872 | tf_op jit(solution)/shard_map/ppermute | solution.py:32
  56.1 0.8 copy-start.7
  56.1 1.0 copy-start.8
  56.2 1.3 copy-start.9
  57.0 0.8 copy-start.10
  57.0 2.1 %collective-permute-start.17 = (bf16[32,8192]{1,0:T(8,128)(2,1)}, bf16[32,8192]{1,0:T(8,128)(2,1)S(1)}, u32[]{:S(2)}, u32[]{:S(2)}) collective-permute-start(bf16[32,8192]{1,0:T(8,128)(2,1)} %collective-permute-done.4.refs_8_), channel_id=1, source_target_pairs={{0,1},{1,0},{2,3},{3,2},{4,5},{5,4},{6,7},{7,6},{8,9},{9,8},{10,11... | collective-permute-start | bytes 1572872 | tf_op jit(solution)/shard_map/ppermute | solution.py:32
  57.2 2.7 %collective-permute-start.18 = (bf16[32,8192]{1,0:T(8,128)(2,1)}, bf16[32,8192]{1,0:T(8,128)(2,1)S(1)}, u32[]{:S(2)}, u32[]{:S(2)}) collective-permute-start(bf16[32,8192]{1,0:T(8,128)(2,1)} %collective-permute-done.5.refs_9_), channel_id=1, source_target_pairs={{0,1},{1,0},{2,3},{3,2},{4,5},{5,4},{6,7},{7,6},{8,9},{9,8},{10,11... | collective-permute-start | bytes 1572872 | tf_op jit(solution)/shard_map/ppermute | solution.py:32
  59.1 0.8 copy-start.11
  59.9 0.8 copy-start.12
  87.2 22.8 %copy-start = (f32[8,2,32,896]{3,2,1,0:T(8,128)S(1)}, f32[8,2,32,896]{3,2,1,0:T(8,128)}, u32[]{:S(2)}) copy-start(f32[8,2,32,896]{3,2,1,0:T(8,128)} %shard_map.30) | copy-start | bytes 5505028
  88.5 12.2 %collective-permute-start.19 = (f32[2,32,896]{2,1,0:T(8,128)S(1)}, f32[2,32,896]{2,1,0:T(8,128)S(1)}, u32[]{:S(2)}, u32[]{:S(2)}) collective-permute-start(f32[2,32,896]{2,1,0:T(8,128)S(1)} %get-tuple-element.54), channel_id=1, source_target_pairs={{0,16},{1,17},{2,18},{3,19},{4,20},{5,21},{6,22},{7,23},{8,24},{9,... | collective-permute-start | bytes 688136 | tf_op jit(solution)/shard_map/ppermute | solution.py:32
  90.5 11.4 %collective-permute-start.23 = (f32[2,32,896]{2,1,0:T(8,128)S(1)}, f32[2,32,896]{2,1,0:T(8,128)S(1)}, u32[]{:S(2)}, u32[]{:S(2)}) collective-permute-start(f32[2,32,896]{2,1,0:T(8,128)S(1)} %get-tuple-element.53), channel_id=1, source_target_pairs={{0,112},{1,113},{2,114},{3,115},{4,116},{5,117},{6,118},{7,119},{8... | collective-permute-start | bytes 688136 | tf_op jit(solution)/shard_map/ppermute | solution.py:32
  101.7 8.4 %collective-permute-start.20 = (f32[2,32,896]{2,1,0:T(8,128)S(1)}, f32[2,32,896]{2,1,0:T(8,128)S(1)}, u32[]{:S(2)}, u32[]{:S(2)}) collective-permute-start(f32[2,32,896]{2,1,0:T(8,128)S(1)} %bitcast_add_fusion.5), channel_id=1, source_target_pairs={{0,16},{1,17},{2,18},{3,19},{4,20},{5,21},{6,22},{7,23},{8,24},{9,... | collective-permute-start | bytes 688136 | tf_op jit(solution)/shard_map/ppermute | solution.py:32
  110.1 6.3 %collective-permute-start.24 = (f32[2,32,896]{2,1,0:T(8,128)S(1)}, f32[2,32,896]{2,1,0:T(8,128)S(1)}, u32[]{:S(2)}, u32[]{:S(2)}) collective-permute-start(f32[2,32,896]{2,1,0:T(8,128)S(1)} %get-tuple-element.51), channel_id=1, source_target_pairs={{0,112},{1,113},{2,114},{3,115},{4,116},{5,117},{6,118},{7,119},{8... | collective-permute-start | bytes 688136 | tf_op jit(solution)/shard_map/ppermute | solution.py:32
  110.4 7.3 %collective-permute-start.21 = (f32[2,32,896]{2,1,0:T(8,128)S(1)}, f32[2,32,896]{2,1,0:T(8,128)S(1)}, u32[]{:S(2)}, u32[]{:S(2)}) collective-permute-start(f32[2,32,896]{2,1,0:T(8,128)S(1)} %get-tuple-element.52), channel_id=1, source_target_pairs={{0,16},{1,17},{2,18},{3,19},{4,20},{5,21},{6,22},{7,23},{8,24},{9,... | collective-permute-start | bytes 688136 | tf_op jit(solution)/shard_map/ppermute | solution.py:32
  117.7 7.3 %collective-permute-start.22 = (f32[2,32,896]{2,1,0:T(8,128)S(1)}, f32[2,32,896]{2,1,0:T(8,128)S(1)}, u32[]{:S(2)}, u32[]{:S(2)}) collective-permute-start(f32[2,32,896]{2,1,0:T(8,128)S(1)} %get-tuple-element.50), channel_id=1, source_target_pairs={{0,16},{1,17},{2,18},{3,19},{4,20},{5,21},{6,22},{7,23},{8,24},{9,... | collective-permute-start | bytes 688136 | tf_op jit(solution)/shard_map/ppermute | solution.py:32
  118.3 6.7 %collective-permute-start.25 = (f32[2,32,896]{2,1,0:T(8,128)S(1)}, f32[2,32,896]{2,1,0:T(8,128)S(1)}, u32[]{:S(2)}, u32[]{:S(2)}) collective-permute-start(f32[2,32,896]{2,1,0:T(8,128)S(1)} %get-tuple-element.49), channel_id=1, source_target_pairs={{0,112},{1,113},{2,114},{3,115},{4,116},{5,117},{6,118},{7,119},{8... | collective-permute-start | bytes 688136 | tf_op jit(solution)/shard_map/ppermute | solution.py:32
  125.1 10.0 %collective-permute-start.27 = (f32[32,896]{1,0:T(8,128)S(1)}, f32[32,896]{1,0:T(8,128)S(1)}, u32[]{:S(2)}, u32[]{:S(2)}) collective-permute-start(f32[32,896]{1,0:T(8,128)S(1)} %get-tuple-element.58), channel_id=1, source_target_pairs={{0,128},{1,129},{2,160},{3,161},{4,132},{5,133},{6,164},{7,165},{8... | collective-permute-start | bytes 344072 | tf_op jit(solution)/shard_map/ppermute | solution.py:32
  128.2 9.4 %collective-permute-start.26 = (f32[32,896]{1,0:T(8,128)S(1)}, f32[32,896]{1,0:T(8,128)S(1)}, u32[]{:S(2)}, u32[]{:S(2)}) collective-permute-start(f32[32,896]{1,0:T(8,128)S(1)} %get-tuple-element.57), channel_id=1, source_target_pairs={{0,0},{1,1},{2,32},{3,33},{4,4},{5,5},{6,36},{7,37},{8,8},{9,9},{1... | collective-permute-start | bytes 344072 | tf_op jit(solution)/shard_map/ppermute | solution.py:32
